TPU v7x, 32 devices: a whole 2x2x4 slice. The times are simulated.
32 devices in a mesh: row: 8 (over y, x, core), col: 4 (over z).
Axes of the slice: x: 2, y: 2, z: 4, core: 2. Of those that a mesh axis runs over, the one named last changes fastest.
Arguments:
- pair: bfloat16 [256, 256, 128], P('row', 'col'), may hold values from -6 to 6
- cotangent: bfloat16 [256, 256, 128], P('row', 'col'), may hold values from -6 to 6
- length: int32 [1], replicated, may hold values from 128 to 256
- norm_gain: float32 [128], replicated, may hold values from 0.1 to 1.9
- norm_bias: float32 [128], replicated, may hold values from -1.5 to 1.5
- left_weight: bfloat16 [128, 256], replicated, may hold values from -0.5 to 0.5
- right_weight: bfloat16 [128, 256], replicated, may hold values from -0.5 to 0.5
- gate_weight: bfloat16 [128, 128], replicated, may hold values from -0.5 to 0.5
- out_gain: float32 [128], replicated, may hold values from 0.1 to 1.9
- out_bias: float32 [128], replicated, may hold values from -2 to 2
- out_weight: bfloat16 [128, 128], replicated, may hold values from -0.5 to 0.5
Outputs:
- update: bfloat16 [256, 256, 128], P('row', 'col')
- grad_pair: bfloat16 [256, 256, 128], P('row', 'col')
- grad_left: float32 [128, 256], replicated
- grad_right: float32 [128, 256], replicated
- grad_gating: float32 [128, 128], replicated
- grad_output: float32 [128, 128], replicated
- grad_norms: float32 [4, 128], replicated
Inputs may be any that keep to these rules, and one draw needn't show every extreme that they name: Tokens at positions 255 down to length are padding.
All inputs are finite; a program needn't handle non-finite values.
Results may differ from a plain program's by a relative error of at most 0.014.
Values may be sent and summed in bfloat16 or wider, within the bound.
No kernel may reach another device: no remote copies, remote signals or barrier semaphores. Data moves between devices by JAX's collectives and lax.ppermute only.
A program may use at most 128 MiB of HBM per device.

v0:
```python
import functools

import jax
import jax.numpy as jnp
from jax import lax
from jax.experimental import pallas as pl
from jax.experimental.pallas import tpu as pltpu
from jax.sharding import PartitionSpec as P

EPS = 1e-05
BOTH = ("row", "col")
LANES = 128
F32, BF16 = jnp.float32, jnp.bfloat16
NN = (((1,), (0,)), ((), ()))
NT = (((1,), (1,)), ((), ()))
TN = (((0,), (0,)), ((), ()))
VMEM = pl.BlockSpec(memory_space=pltpu.VMEM)
SMEM = pl.BlockSpec(memory_space=pltpu.SMEM)


def dot(a, b, dims=NN):
    return lax.dot_general(a, b, dims, preferred_element_type=F32)


def call(body, outs, scratch, name, flops, moved):
    return pl.pallas_call(
        body,
        out_shape=tuple(jax.ShapeDtypeStruct(s, d) for s, d in outs),
        out_specs=tuple(VMEM for _ in outs),
        scratch_shapes=scratch,
        name=name,
        compiler_params=pltpu.CompilerParams(vmem_limit_bytes=24 * 2**20),
        cost_estimate=pl.CostEstimate(flops=flops, bytes_accessed=moved, transcendentals=0),
    )


def exchange(blocks):
    return lax.all_to_all(blocks, BOTH, split_axis=0, concat_axis=0, tiled=True)


def swap_halves(a, b):
    half = LANES // 2
    first = jnp.concatenate([a[:, :half], b[:, :half]], axis=1)
    second = jnp.concatenate([a[:, half:], b[:, half:]], axis=1)
    return first, second


def column(row):
    return jnp.broadcast_to(row, (LANES, row.shape[1])).T


def flip(weight):
    return weight.astype(F32).T.astype(BF16)


def token_tile(ref, p, half):
    return jnp.concatenate([ref[p], ref[half + p]], axis=0)


def mask_row(info, p, half, cols):
    lane = lax.broadcasted_iota(jnp.int32, (1, LANES), 1)
    second = (lane >= cols).astype(jnp.int32)
    row = info[0] + p + half * second
    col = info[1] + lane - cols * second
    return ((row < info[2]) & (col < info[2])).astype(F32)


def normal(x, axis):
    center = x - jnp.mean(x, axis=axis, keepdims=True)
    inverse = lax.rsqrt(jnp.mean(center * center, axis=axis, keepdims=True) + EPS)
    return center * inverse, inverse


def project(half, hidden, info, pair, gain, bias, lw, rw, send, nt_out, wt, gb, ls, rs):
    n_dev, _, per, _ = send.shape
    cols = pair.shape[1]
    wt[0] = flip(lw[...])
    wt[1] = flip(rw[...])
    gb[0] = column(gain[...])
    gb[1] = column(bias[...])

    def step(p, carry):
        x = token_tile(pair, p, half).astype(F32).T
        hat, _ = normal(x, 0)
        nt = (hat * gb[0] + gb[1]).astype(BF16)
        nt_out[:, pl.ds(pl.multiple_of(p * LANES, LANES), LANES)] = nt
        mask = mask_row(info, p, half, cols)
        for side, scr in ((0, ls), (1, rs)):
            proj = dot(wt[side], nt)
            act = mask * jax.nn.sigmoid(proj[hidden:]) * proj[:hidden]
            scr[pl.ds(p, hidden, stride=half), :] = act
        return carry

    lax.fori_loop(0, half, step, 0, unroll=2)

    def pack(d, carry):
        at = pl.ds(pl.multiple_of(d * per, per), per)
        send[d, 0] = ls[at, :].astype(BF16)
        send[d, 1] = rs[at, :].astype(BF16)
        return carry

    lax.fori_loop(0, n_dev, pack, 0, unroll=4)


def prepare(half, hidden, info, pair, cot, nt_in, lw, rw, gw, gate_out, cot_out, coef, hat_out, scale_out, wt, gwt):
    cols = pair.shape[1]
    wt[0] = flip(lw[...])
    wt[1] = flip(rw[...])
    gwt[...] = flip(gw[...])

    def step(p, carry):
        at = pl.ds(pl.multiple_of(p * LANES, LANES), LANES)
        x = token_tile(pair, p, half).astype(F32).T
        hat, inverse = normal(x, 0)
        hat_out[:, at] = hat
        scale_out[:, at] = jnp.broadcast_to(inverse, (8, LANES))
        cot_out[:, at] = token_tile(cot, p, half).astype(F32).T
        nt = nt_in[:, at]
        gate_out[:, at] = jax.nn.sigmoid(dot(gwt[...], nt))
        mask = mask_row(info, p, half, cols)
        for side in (0, 1):
            proj = dot(wt[side], nt)
            sig = jax.nn.sigmoid(proj[hidden:])
            coef[2 * side, :, at] = mask * sig
            coef[2 * side + 1, :, at] = mask * proj[:hidden] * sig * (1.0 - sig)
        return carry

    lax.fori_loop(0, half, step, 0, unroll=2)


def gather_whole(n_row, n_col, half, read, write):
    for r in range(n_row):
        for m in range(n_col // 2):
            first, second = swap_halves(read(r * n_col + 2 * m), read(r * n_col + 2 * m + 1))
            write(2 * r * half, m * LANES, first)
            write((2 * r + 1) * half, m * LANES, second)


def scatter_tiles(n_row, n_col, half, whole, write):
    for r in range(n_row):
        for m in range(n_col // 2):
            at = slice(m * LANES, (m + 1) * LANES)
            a = whole[2 * r * half : (2 * r + 1) * half, at]
            b = whole[(2 * r + 1) * half : (2 * r + 2) * half, at]
            first, second = swap_halves(a, b)
            write(r * n_col + 2 * m, first)
            write(r * n_col + 2 * m + 1, second)


def multiply(n_row, n_col, half, recv, send, left, right, acc):
    def step(h, carry):
        at = pl.ds(pl.multiple_of(h * half, half), half)
        for side, out in ((0, left), (1, right)):

            def write(row, lane, block, out=out):
                out[h, row : row + half, lane : lane + LANES] = block

            gather_whole(n_row, n_col, half, lambda d, side=side: recv[d, side, at, :], write)
        acc[...] = dot(left[h], right[h], NT)

        def put(d, block):
            send[d, at, :] = block.astype(BF16)

        scatter_tiles(n_row, n_col, half, acc, put)
        return carry

    lax.fori_loop(0, left.shape[0], step, 0)


def multiply_back(n_row, n_col, half, recv, left, right, send, grad, acc):
    def step(h, carry):
        at = pl.ds(pl.multiple_of(h * half, half), half)

        def write(row, lane, block):
            grad[row : row + half, lane : lane + LANES] = block

        gather_whole(n_row, n_col, half, lambda d: recv[d, at, :], write)
        acc[0] = dot(grad[...], right[h], NN)
        acc[1] = dot(grad[...], left[h], TN)
        for side in (0, 1):

            def put(d, block, side=side):
                send[d, side, at, :] = block.astype(BF16)

            scatter_tiles(n_row, n_col, half, acc.at[side], put)
        return carry

    lax.fori_loop(0, left.shape[0], step, 0)


def unpack(recv, scr, side=None):
    n_dev, per = recv.shape[0], recv.shape[-2]

    def step(d, carry):
        at = pl.ds(pl.multiple_of(d * per, per), per)
        block = recv[d] if side is None else recv[d, side]
        scr[at, :] = block.astype(F32)
        return carry

    lax.fori_loop(0, n_dev, step, 0, unroll=4)


def middle(half, hidden, recv, gate_in, cot_in, gain, bias, ow, send, upd, og_out, gg_out, tn_out, sums, scr, owt, gb):
    n_dev, per, _ = send.shape
    unpack(recv, scr)
    owt[...] = flip(ow[...])
    gb[0] = column(gain[...])
    gb[1] = column(bias[...])
    sums[...] = jnp.zeros_like(sums)

    def step(p, carry):
        at = pl.ds(pl.multiple_of(p * LANES, LANES), LANES)
        rows = pl.ds(p, hidden, stride=half)
        hat, scale = normal(scr[rows, :], 0)
        tn = (hat * gb[0] + gb[1]).astype(BF16)
        tn_out[:, at] = tn
        outer = dot(owt[...], tn)
        gate = gate_in[:, at]
        up = cot_in[:, at]
        upd[:, at] = gate * outer
        og = (up * gate).astype(BF16)
        og_out[:, at] = og
        gg_out[:, at] = (up * outer * gate * (1.0 - gate)).astype(BF16)
        tg = dot(ow[...], og)
        sums[0] += tg * hat
        sums[1] += tg
        hg = tg * gb[0]
        back = hg - jnp.mean(hg, axis=0, keepdims=True)
        back = back - hat * jnp.mean(hg * hat, axis=0, keepdims=True)
        scr[rows, :] = scale * back
        return carry

    lax.fori_loop(0, half, step, 0, unroll=2)

    def pack(d, carry):
        at = pl.ds(pl.multiple_of(d * per, per), per)
        send[d] = scr[at, :].astype(BF16)
        return carry

    lax.fori_loop(0, n_dev, pack, 0, unroll=4)


def fold(x):
    return jnp.sum(x.T, axis=0, keepdims=True)


def settle(half, upd, og, gg, tn, nt, sums, update, early, norms):
    def step(p, carry):
        at = pl.ds(pl.multiple_of(p * LANES, LANES), LANES)
        tile = upd[:, at].T.astype(BF16)
        cols = update.shape[1]
        update[p] = tile[:cols]
        update[half + p] = tile[cols:]
        return carry

    lax.fori_loop(0, half, step, 0, unroll=2)
    early[0] = dot(nt[...], gg[...], NT)
    early[1] = dot(tn[...], og[...], NT)
    norms[0:1] = fold(sums[0])
    norms[1:2] = fold(sums[1])


def finish(half, hidden, recv, coef, nt, gg, hat, lw, rw, gw, early, early_norms, parts, ng_out, scr, comb, sums):
    for side in (0, 1):
        unpack(recv, scr.at[side], side)
    sums[...] = jnp.zeros_like(sums)

    def step(p, carry):
        at = pl.ds(pl.multiple_of(p * LANES, LANES), LANES)
        rows = pl.ds(p, hidden, stride=half)
        ng = dot(gw[...], gg[:, at])
        for side, w in ((0, lw), (1, rw)):
            part = scr[side, rows, :]
            both = jnp.concatenate(
                [part * coef[2 * side, :, at], part * coef[2 * side + 1, :, at]], axis=0
            ).astype(BF16)
            comb[side, :, at] = both
            ng = ng + dot(w[...], both)
        ng_out[:, at] = ng
        sums[0] += ng * hat[:, at]
        sums[1] += ng
        return carry

    lax.fori_loop(0, half, step, 0, unroll=2)
    c = nt.shape[0]
    parts[...] = jnp.zeros_like(parts)
    for side in (0, 1):
        grad = dot(nt[...], comb[side], NT)
        parts[2 * side * c : (2 * side + 1) * c] = grad[:, :hidden].astype(BF16)
        parts[(2 * side + 1) * c : (2 * side + 2) * c] = grad[:, hidden:].astype(BF16)
    parts[4 * c : 5 * c] = early[0].astype(BF16)
    parts[5 * c : 5 * c + hidden] = early[1].astype(BF16)
    exact = jnp.concatenate([fold(sums[0]), fold(sums[1]), early_norms[0:2]], axis=0)
    high = exact.astype(BF16)
    low = (exact - high.astype(F32)).astype(BF16)
    base = 5 * c + hidden
    parts[base : base + 8] = jnp.concatenate([high, low], axis=0)


def add_up(scale, holder, device, recv, send):
    n_dev, share, _ = recv.shape
    mine = scale * jnp.sum(recv[...].astype(F32), axis=0)
    exact = mine[0:4] + mine[4:8]
    high = exact.astype(BF16).astype(F32)
    pairs = jnp.concatenate([high, exact - high], axis=0)
    if share > 8:
        pairs = jnp.concatenate([pairs, mine[8:]], axis=0)
    keep = (device[0] == holder).astype(F32)
    result = (keep * pairs + (1.0 - keep) * mine).astype(BF16)
    for d in range(n_dev):
        send[d] = result


def close(half, ng, hat, scale, gain, grad_pair, gb):
    gb[...] = column(gain[...])
    cols = grad_pair.shape[1]

    def step(p, carry):
        at = pl.ds(pl.multiple_of(p * LANES, LANES), LANES)
        q = ng[:, at] * gb[...]
        h = hat[:, at]
        back = q - jnp.mean(q, axis=0, keepdims=True)
        back = back - h * jnp.mean(q * h, axis=0, keepdims=True)
        tile = (scale[0:1, at] * back).T.astype(BF16)
        grad_pair[p] = tile[:cols]
        grad_pair[half + p] = tile[cols:]
        return carry

    lax.fori_loop(0, half, step, 0, unroll=2)


def per_device(
    pair,
    cotangent,
    length,
    norm_gain,
    norm_bias,
    left_weight,
    right_weight,
    gate_weight,
    out_gain,
    out_bias,
    out_weight,
):
    n_row = lax.axis_size("row")
    n_col = lax.axis_size("col")
    n_dev = n_row * n_col
    rows_dev, cols_dev, c = pair.shape
    tokens = rows_dev * n_row
    hidden = out_weight.shape[0]
    own = hidden // n_dev
    half = rows_dev * cols_dev // LANES
    wide = half * LANES
    per = own * half
    assert 2 * cols_dev == LANES and rows_dev == 2 * half and c == LANES and hidden == LANES
    info = jnp.stack(
        [
            lax.axis_index("row").astype(jnp.int32) * rows_dev,
            lax.axis_index("col").astype(jnp.int32) * cols_dev,
            length[0],
        ]
    )
    gain, bias = norm_gain[None], norm_bias[None]
    o_gain, o_bias = out_gain[None], out_bias[None]
    vm = pltpu.VMEM
    sq = (c, LANES)

    send, nt = call(
        functools.partial(project, half, hidden),
        [((n_dev, 2, per, LANES), BF16), ((c, wide), BF16)],
        [vm((2, 2 * hidden, c), BF16), vm((2,) + sq, F32)] + [vm((hidden * half, LANES), F32)] * 2,
        "project", 300 * 10**6, 3 * 2**20,
    )(info, pair, gain, bias, left_weight, right_weight)
    both = exchange(send)
    gate, cot, coef, hat, scale = call(
        functools.partial(prepare, half, hidden),
        [((c, wide), F32), ((c, wide), F32), ((4, hidden, wide), F32), ((c, wide), F32), ((8, wide), F32)],
        [vm((2, 2 * hidden, c), BF16), vm((c, c), BF16)],
        "prepare", 400 * 10**6, 9 * 2**20,
    )(info, pair, cotangent, nt, left_weight, right_weight, gate_weight)
    send, left, right = call(
        functools.partial(multiply, n_row, n_col, half),
        [((n_dev, per, LANES), BF16), ((own, tokens, tokens), BF16), ((own, tokens, tokens), BF16)],
        [vm((tokens, tokens), F32)],
        "multiply", 200 * 10**6, 3 * 2**20,
    )(both)
    tri = exchange(send)
    send, upd, og, gg, tn, sums = call(
        functools.partial(middle, half, hidden),
        [((n_dev, per, LANES), BF16), ((c, wide), F32)] + [((c, wide), BF16)] * 3 + [((2,) + sq, F32)],
        [vm((hidden * half, LANES), F32), vm((c, hidden), BF16), vm((2,) + sq, F32)],
        "middle", 200 * 10**6, 6 * 2**20,
    )(tri, gate, cot, o_gain, o_bias, out_weight)
    grad = exchange(send)
    update, early, early_norms = call(
        functools.partial(settle, half),
        [((rows_dev, cols_dev, c), BF16), ((2,) + sq, F32), ((8, LANES), F32)],
        [],
        "settle", 200 * 10**6, 4 * 2**20,
    )(upd, og, gg, tn, nt, sums)
    (send,) = call(
        functools.partial(multiply_back, n_row, n_col, half),
        [((n_dev, 2, per, LANES), BF16)],
        [vm((tokens, tokens), BF16), vm((2, tokens, tokens), F32)],
        "multiply_back", 300 * 10**6, 3 * 2**20,
    )(grad, left, right)
    back = exchange(send)
    used = 5 * c + hidden + 8
    assert (5 * c + hidden) % 8 == 0
    share = -(-used // (n_dev * 8)) * 8
    while (5 * c + hidden) % share:
        share += 8
    device = (lax.axis_index("row") * n_col + lax.axis_index("col")).astype(jnp.int32)[None]
    parts, ng = call(
        functools.partial(finish, half, hidden),
        [((n_dev * share, LANES), BF16), ((c, wide), F32)],
        [vm((2, hidden * half, LANES), F32), vm((2, 2 * hidden, wide), BF16), vm((2,) + sq, F32)],
        "finish", 500 * 10**6, 10 * 2**20,
    )(back, coef, nt, gg, hat, left_weight, right_weight, gate_weight, early, early_norms)
    (send,) = call(
        functools.partial(add_up, 1.0 / tokens, (5 * c + hidden) // share),
        [((n_dev, share, LANES), BF16)],
        [],
        "add_up", 10**6, 2**19,
    )(device, exchange(parts.reshape(n_dev, share, LANES)))
    totals = exchange(send).reshape(n_dev * share, LANES).astype(F32)
    (grad_pair,) = call(
        functools.partial(close, half),
        [((rows_dev, cols_dev, c), BF16)],
        [vm(sq, F32)],
        "close", 50 * 10**6, 3 * 2**20,
    )(ng, hat, scale, gain)
    base = 5 * c + hidden
    return (
        update,
        grad_pair,
        jnp.concatenate([totals[:c], totals[c : 2 * c]], axis=1),
        jnp.concatenate([totals[2 * c : 3 * c], totals[3 * c : 4 * c]], axis=1),
        totals[4 * c : 5 * c],
        totals[5 * c : base],
        totals[base : base + 4] + totals[base + 4 : base + 8],
    )


def solution(mesh):
    return jax.shard_map(
        per_device,
        mesh=mesh,
        in_specs=(P("row", "col", None), P("row", "col", None)) + (P(),) * 9,
        out_specs=(P("row", "col", None), P("row", "col", None), P(), P(), P(), P(), P()),
        check_vma=False,
    )
```

profile of v0, /device:TPU:0, one launch (start us, length us, event | category | flops | bytes accessed | tf_op | source)
XLA Modules:
  0.0 160.4 jit_solution(10825797950160541800)
XLA Ops:
  1.3 0.1 pad_add_fusion.info
  1.4 1.0 copy-done.17
  2.4 0.8 copy-done.20
  3.3 0.8 copy-done.22
  4.1 0.7 copy-done.30
  4.8 0.7 copy-done.32
  5.4 0.0 copy-start.27
  5.5 4.1 %project.1 = (bf16[32,2,64,128]{3,2,1,0:T(8,128)(2,1)S(1)}, bf16[128,2048]{1,0:T(8,128)(2,1)S(1)}) custom-call(s32[3]{0:T(128)S(1)} %pad_add_fusion.info, bf16[32,64,128]{2,1,0:T(8,128)(2,1)S(1)} %copy-done.17, f32[1,128]{1,0:T(1,128)S(1)} %bitcast.17, f32[1,128]{1,0:T(1,128)S(1)} %bitcast.19, bf16[128,256]{1,0:T(8,128)(2,1)S(1)} %copy-done.20, ...), custom_call_target="tpu_custom_call" | custom-call | flops 300000000 | bytes 3145728 | tf_op jit(solution)/shard_map/project/pallas_call | solution.py:368
  9.6 32.1 %all_to_all.30.recv = bf16[32,2,64,128]{3,2,1,0:T(8,128)(2,1)S(1)} all-to-all(bf16[32,2,64,128]{3,2,1,0:T(8,128)(2,1)S(1)} %get-tuple-element.28), channel_id=1, replica_groups=mesh['row'=8,'col'=4] {'row','col'}, dimensions={0} | all-to-all | bytes 2097152 | tf_op jit(solution)/shard_map/all_to_all | solution.py:38
  41.6 2.3 %multiply.1 = (bf16[32,64,128]{2,1,0:T(8,128)(2,1)}, bf16[4,256,256]{2,1,0:T(8,128)(2,1)S(1)}, bf16[4,256,256]{2,1,0:T(8,128)(2,1)S(1)}) custom-call(bf16[32,2,64,128]{3,2,1,0:T(8,128)(2,1)S(1)} %all_to_all.30.recv), custom_call_target="tpu_custom_call" | custom-call | flops 200000000 | bytes 3145728 | tf_op jit(solution)/shard_map/multiply/pallas_call | solution.py:381
  44.0 0.8 copy-done.11
  44.8 4.5 %all-to-all-start.1 = ((bf16[32,64,128]{2,1,0:T(8,128)(2,1)}), bf16[32,64,128]{2,1,0:T(8,128)(2,1)S(1)}, u32[]{:S(2)}, u32[]{:S(2)}) async-start(bf16[32,64,128]{2,1,0:T(8,128)(2,1)} %get-tuple-element.29), calls=%async_computation.1 | async-start | bytes 1048576 | tf_op jit(solution)/shard_map/all_to_all | solution.py:38
  49.4 0.0 copy-start.19
  49.4 1.0 copy-done.19
  50.4 2.5 %prepare.1 = (f32[128,2048]{1,0:T(8,128)S(1)}, f32[128,2048]{1,0:T(8,128)S(1)}, f32[4,128,2048]{2,1,0:T(8,128)S(1)}, f32[128,2048]{1,0:T(8,128)S(1)}, f32[8,2048]{1,0:T(8,128)S(1)}) custom-call(s32[3]{0:T(128)S(1)} %pad_add_fusion.info, bf16[32,64,128]{2,1,0:T(8,128)(2,1)S(1)} %copy-done.18, bf16[32,64,128]{2,1,0:T(8,128)(2,1)S(1)} %copy-done.19, ...), custom_call_target="tpu_custom_call" | custom-call | flops 400000000 | bytes 9437184 | tf_op jit(solution)/shard_map/prepare/pallas_call | solution.py:375
  52.9 2.0 %copy-done = f32[4,128,2048]{2,1,0:T(8,128)} copy-done((f32[4,128,2048]{2,1,0:T(8,128)}, f32[4,128,2048]{2,1,0:T(8,128)S(1)}, u32[]{:S(2)}) %copy-start) | copy-done | bytes 4194328
  54.9 1.0 copy-done.5
  55.9 1.0 copy-done.7
  56.9 6.7 %all-to-all-done.1.recv = bf16[32,64,128]{2,1,0:T(8,128)(2,1)S(1)} async-done(((bf16[32,64,128]{2,1,0:T(8,128)(2,1)}), bf16[32,64,128]{2,1,0:T(8,128)(2,1)S(1)}, u32[]{:S(2)}, u32[]{:S(2)}) %all-to-all-start.1) | async-done | bytes 524320 | tf_op jit(solution)/shard_map/all_to_all | solution.py:38
  63.6 1.2 copy-done.6
  64.8 1.2 copy-done.8
  66.0 3.1 %middle.1 = (bf16[32,64,128]{2,1,0:T(8,128)(2,1)S(1)}, f32[128,2048]{1,0:T(8,128)S(1)}, bf16[128,2048]{1,0:T(8,128)(2,1)S(1)}, bf16[128,2048]{1,0:T(8,128)(2,1)S...) custom-call(bf16[32,64,128]{2,1,0:T(8,128)(2,1)S(1)} %all-to-all-done.1.recv, f32[128,2048]{1,0:T(8,128)S(1)} %copy-done.6, ...), custom_call_target="tpu_custom_call" | custom-call | flops 200000000 | bytes 6291456 | tf_op jit(solution)/shard_map/middle/pallas_call | solution.py:388
  69.2 0.8 copy-done.13
  69.9 0.8 copy-done.15
  70.7 18.2 %all_to_all.31.recv = bf16[32,64,128]{2,1,0:T(8,128)(2,1)S(1)} all-to-all(bf16[32,64,128]{2,1,0:T(8,128)(2,1)S(1)} %get-tuple-element.39), channel_id=1, replica_groups=mesh['row'=8,'col'=4] {'row','col'}, dimensions={0} | all-to-all | bytes 1048576 | tf_op jit(solution)/shard_map/all_to_all | solution.py:38
  89.0 1.0 copy-done.12
  90.0 1.6 %multiply_back.1 = bf16[32,2,64,128]{3,2,1,0:T(8,128)(2,1)S(1)} custom-call(bf16[32,64,128]{2,1,0:T(8,128)(2,1)S(1)} %all_to_all.31.recv, bf16[4,256,256]{2,1,0:T(8,128)(2,1)S(1)} %get-tuple-element.40.left, bf16[4,256,256]{2,1,0:T(8,128)(2,1)S(1)} %copy-done.12), custom_call_target="tpu_custom_call" | custom-call | flops 300000000 | bytes 3145728 | tf_op jit(solution)/shard_map/multiply_back/pallas_call | solution.py:401
  91.7 1.0 copy-done.2
  92.6 4.2 %all-to-all-start.3 = ((bf16[32,2,64,128]{3,2,1,0:T(8,128)(2,1)}), bf16[32,2,64,128]{3,2,1,0:T(8,128)(2,1)S(1)}, u32[]{:S(2)}, u32[]{:S(2)}) async-start(bf16[32,2,64,128]{3,2,1,0:T(8,128)(2,1)} %copy-done.2), calls=%async_computation.3 | async-start | bytes 2097152 | tf_op jit(solution)/shard_map/all_to_all | solution.py:38
  96.8 1.2 copy-done.4
  98.0 1.0 copy-done.14
  99.1 1.0 copy-done.16
  100.1 0.9 copy-done.26
  101.0 1.6 %settle.1 = (bf16[32,64,128]{2,1,0:T(8,128)(2,1)}, f32[2,128,128]{2,1,0:T(8,128)S(1)}, f32[8,128]{1,0:T(8,128)S(1)}) custom-call(f32[128,2048]{1,0:T(8,128)S(1)} %copy-done.4, bf16[128,2048]{1,0:T(8,128)(2,1)S(1)} %copy-done.14, bf16[128,2048]{1,0:T(8,128)(2,1)S(1)} %get-tuple-element.35.gg, bf16[128,2048]{1,0:T(8,128)(2,1)S(1)} %copy-done.16, ...), custom_call_target="tpu_custom_call" | custom-call | flops 200000000 | bytes 4194304 | tf_op jit(solution)/shard_map/settle/pallas_call | solution.py:395
  102.7 19.1 %all-to-all-done.3.recv = bf16[32,2,64,128]{3,2,1,0:T(8,128)(2,1)S(1)} async-done(((bf16[32,2,64,128]{3,2,1,0:T(8,128)(2,1)}), bf16[32,2,64,128]{3,2,1,0:T(8,128)(2,1)S(1)}, u32[]{:S(2)}, u32[]{:S(2)}) %all-to-all-start.3) | async-done | bytes 1048608 | tf_op jit(solution)/shard_map/all_to_all | solution.py:38
  121.7 2.2 %copy-done.1 = f32[4,128,2048]{2,1,0:T(8,128)S(1)} copy-done((f32[4,128,2048]{2,1,0:T(8,128)S(1)}, f32[4,128,2048]{2,1,0:T(8,128)}, u32[]{:S(2)}) %copy-start.1) | copy-done | bytes 4194328
  123.9 5.0 %finish.1 = (bf16[1024,128]{1,0:T(8,128)(2,1)}, f32[128,2048]{1,0:T(8,128)S(1)}) custom-call(bf16[32,2,64,128]{3,2,1,0:T(8,128)(2,1)S(1)} %all-to-all-done.3.recv, f32[4,128,2048]{2,1,0:T(8,128)S(1)} %copy-done.1, bf16[128,2048]{1,0:T(8,128)(2,1)S(1)} %get-tuple-element.30.nt_in.nt, bf16[128,2048]{1,0:T(8,128)(2,1)S(1)} %get-tuple-element.35.gg, ...), custom_call_target="tpu_custom_call" | custom-call | flops 500000000 | bytes 10485760 | tf_op jit(solution)/shard_map/finish/pallas_call | solution.py:414
  128.9 1.0 copy-done.9
  129.9 4.5 %all-to-all-start.4 = ((bf16[32,32,128]{2,1,0:T(8,128)(2,1)}), bf16[32,32,128]{2,1,0:T(8,128)(2,1)S(1)}, u32[]{:S(2)}, u32[]{:S(2)}) async-start(bf16[32,32,128]{2,1,0:T(8,128)(2,1)} %bitcast.7), calls=%async_computation.4 | async-start | bytes 524288 | tf_op jit(solution)/shard_map/all_to_all | solution.py:38
  134.5 10.2 %all-to-all-done.4.recv = bf16[32,32,128]{2,1,0:T(8,128)(2,1)S(1)} async-done(((bf16[32,32,128]{2,1,0:T(8,128)(2,1)}), bf16[32,32,128]{2,1,0:T(8,128)(2,1)S(1)}, u32[]{:S(2)}, u32[]{:S(2)}) %all-to-all-start.4) | async-done | bytes 262176 | tf_op jit(solution)/shard_map/all_to_all | solution.py:38
  144.7 0.8 add_up.1
  145.5 2.7 %all-to-all-start.5 = ((bf16[32,32,128]{2,1,0:T(8,128)(2,1)}), bf16[32,32,128]{2,1,0:T(8,128)(2,1)S(1)}, u32[]{:S(2)}, u32[]{:S(2)}) async-start(bf16[32,32,128]{2,1,0:T(8,128)(2,1)} %add_up.1), calls=%async_computation.5 | async-start | bytes 524288 | tf_op jit(solution)/shard_map/all_to_all | solution.py:38
  148.2 1.2 copy-done.10
  149.4 2.1 %close.1 = bf16[32,64,128]{2,1,0:T(8,128)(2,1)} custom-call(f32[128,2048]{1,0:T(8,128)S(1)} %copy-done.10, f32[128,2048]{1,0:T(8,128)S(1)} %get-tuple-element.43.hat, f32[8,2048]{1,0:T(8,128)S(1)} %get-tuple-element.47.scale, f32[1,128]{1,0:T(1,128)S(1)} %bitcast.18), custom_call_target="tpu_custom_call" | custom-call | flops 50000000 | bytes 3145728 | tf_op jit(solution)/shard_map/close/pallas_call | solution.py:427
  151.5 6.9 %all-to-all-done.5 = bf16[32,32,128]{2,1,0:T(8,128)(2,1)S(1)} async-done(((bf16[32,32,128]{2,1,0:T(8,128)(2,1)}), bf16[32,32,128]{2,1,0:T(8,128)(2,1)S(1)}, u32[]{:S(2)}, u32[]{:S(2)}) %all-to-all-start.5) | async-done | bytes 262176 | tf_op jit(solution)/shard_map/all_to_all | solution.py:38
  158.4 0.6 slice_add_fusion
  159.0 0.7 fusion
  159.7 0.7 pad_maximum_fusion
  (42 shorter events, 0.1 us)
Async XLA Ops:
  0.6 62.9 %copy-start.29 = (f32[128]{0:T(128)S(1)}, f32[128]{0:T(128)}, u32[]{:S(2)}) copy-start(f32[128]{0:T(128)} %param.20) | copy-start | bytes 1540
  0.6 62.9 %copy-start.28 = (f32[128]{0:T(128)S(1)}, f32[128]{0:T(128)}, u32[]{:S(2)}) copy-start(f32[128]{0:T(128)} %param.19) | copy-start | bytes 1540
  1.4 1.0 copy-start.17
  2.4 0.8 copy-start.20
  3.3 0.8 copy-start.22
  4.1 0.7 copy-start.30
  4.8 0.7 copy-start.32
  5.4 43.9 %copy-start.18 = (bf16[32,64,128]{2,1,0:T(8,128)(2,1)S(1)}, bf16[32,64,128]{2,1,0:T(8,128)(2,1)}, u32[]{:S(2)}) copy-start(bf16[32,64,128]{2,1,0:T(8,128)(2,1)} %pair.3) | copy-start | bytes 1572868
  5.4 43.9 %copy-start.21 = (bf16[128,256]{1,0:T(8,128)(2,1)S(1)}, bf16[128,256]{1,0:T(8,128)(2,1)}, u32[]{:S(2)}) copy-start(bf16[128,256]{1,0:T(8,128)(2,1)} %lw.5) | copy-start | bytes 196612
  5.4 43.9 %copy-start.23 = (bf16[128,256]{1,0:T(8,128)(2,1)S(1)}, bf16[128,256]{1,0:T(8,128)(2,1)}, u32[]{:S(2)}) copy-start(bf16[128,256]{1,0:T(8,128)(2,1)} %rw.5) | copy-start | bytes 196612
  5.4 43.9 %copy-start.24 = (bf16[128,128]{1,0:T(8,128)(2,1)S(1)}, bf16[128,128]{1,0:T(8,128)(2,1)}, u32[]{:S(2)}) copy-start(bf16[128,128]{1,0:T(8,128)(2,1)} %gw.3) | copy-start | bytes 98308
  5.4 58.1 %copy-start.27 = (bf16[128,128]{1,0:T(8,128)(2,1)S(1)}, bf16[128,128]{1,0:T(8,128)(2,1)}, u32[]{:S(2)}) copy-start(bf16[128,128]{1,0:T(8,128)(2,1)} %ow.1) | copy-start | bytes 98308
  44.0 0.8 copy-start.11
  44.8 18.8 %all-to-all-start.1 = ((bf16[32,64,128]{2,1,0:T(8,128)(2,1)}), bf16[32,64,128]{2,1,0:T(8,128)(2,1)S(1)}, u32[]{:S(2)}, u32[]{:S(2)}) async-start(bf16[32,64,128]{2,1,0:T(8,128)(2,1)} %get-tuple-element.29), calls=%async_computation.1 | async-start | bytes 1048576 | tf_op jit(solution)/shard_map/all_to_all | solution.py:38
  49.4 1.0 copy-start.19
  52.9 2.0 %copy-start = (f32[4,128,2048]{2,1,0:T(8,128)}, f32[4,128,2048]{2,1,0:T(8,128)S(1)}, u32[]{:S(2)}) copy-start(f32[4,128,2048]{2,1,0:T(8,128)S(1)} %get-tuple-element.42.coef) | copy-start | bytes 12582916
  54.9 1.0 copy-start.5
  55.9 1.0 copy-start.7
  63.6 1.2 copy-start.6
  64.8 1.2 copy-start.8
  69.1 0.8 copy-start.13
  69.9 0.8 copy-start.15
  70.7 18.2 %copy-start.3 = (f32[128,2048]{1,0:T(8,128)}, f32[128,2048]{1,0:T(8,128)S(1)}, u32[]{:S(2)}) copy-start(f32[128,2048]{1,0:T(8,128)S(1)} %get-tuple-element.33.upd) | copy-start | bytes 3145732
  70.7 26.1 %copy-start.25 = (f32[2,128,128]{2,1,0:T(8,128)}, f32[2,128,128]{2,1,0:T(8,128)S(1)}, u32[]{:S(2)}) copy-start(f32[2,128,128]{2,1,0:T(8,128)S(1)} %get-tuple-element.37.sums) | copy-start | bytes 393220
  89.0 1.0 copy-start.12
  91.6 1.0 copy-start.2
  92.6 29.1 %all-to-all-start.3 = ((bf16[32,2,64,128]{3,2,1,0:T(8,128)(2,1)}), bf16[32,2,64,128]{3,2,1,0:T(8,128)(2,1)S(1)}, u32[]{:S(2)}, u32[]{:S(2)}) async-start(bf16[32,2,64,128]{3,2,1,0:T(8,128)(2,1)} %copy-done.2), calls=%async_computation.3 | async-start | bytes 2097152 | tf_op jit(solution)/shard_map/all_to_all | solution.py:38
  96.8 1.2 copy-start.4
  98.0 1.0 copy-start.14
  99.1 1.0 copy-start.16
  100.1 0.9 copy-start.26
  121.7 2.2 %copy-start.1 = (f32[4,128,2048]{2,1,0:T(8,128)S(1)}, f32[4,128,2048]{2,1,0:T(8,128)}, u32[]{:S(2)}) copy-start(f32[4,128,2048]{2,1,0:T(8,128)} %copy-done) | copy-start | bytes 12582916
  123.9 24.2 %copy-start.31 = (f32[128]{0:T(128)S(1)}, f32[128]{0:T(128)}, u32[]{:S(2)}) copy-start(f32[128]{0:T(128)} %param.14) | copy-start | bytes 1540
  128.9 1.0 copy-start.9
  129.9 14.8 %all-to-all-start.4 = ((bf16[32,32,128]{2,1,0:T(8,128)(2,1)}), bf16[32,32,128]{2,1,0:T(8,128)(2,1)S(1)}, u32[]{:S(2)}, u32[]{:S(2)}) async-start(bf16[32,32,128]{2,1,0:T(8,128)(2,1)} %bitcast.7), calls=%async_computation.4 | async-start | bytes 524288 | tf_op jit(solution)/shard_map/all_to_all | solution.py:38
  145.5 12.9 %all-to-all-start.5 = ((bf16[32,32,128]{2,1,0:T(8,128)(2,1)}), bf16[32,32,128]{2,1,0:T(8,128)(2,1)S(1)}, u32[]{:S(2)}, u32[]{:S(2)}) async-start(bf16[32,32,128]{2,1,0:T(8,128)(2,1)} %add_up.1), calls=%async_computation.5 | async-start | bytes 524288 | tf_op jit(solution)/shard_map/all_to_all | solution.py:38
  148.2 1.2 copy-start.10
where the time goes:
time: 161 us; the launch traced here: 160 us
  blocking collectives  50.3 us (31%)
  waiting for transfers between devices  42.8 us (27%)
  local copies, waits for them, and re-layouts  25.1 us (16%)
  Pallas kernels  23.3 us (14%)
  starting transfers between devices  15.9 us (10%)
    all_to_all x2, blocking collectives, exchange(): return lax.all_to_all(blocks, BOTH, split_axis=0, concat_axis=0, tiled=True)  50.3 us
    all_to_all x4, waiting for transfers between devices, exchange(): return lax.all_to_all(blocks, BOTH, split_axis=0, concat_axis=0, tiled=True)  42.8 us
    unnamed x66, local copies, waits for them, and re-layouts  24.4 us
    all_to_all x4, starting transfers between devices, exchange(): return lax.all_to_all(blocks, BOTH, split_axis=0, concat_axis=0, tiled=True)  15.9 us
    pallas_call x1, Pallas kernels, per_device(): call(functools.partial(finish, half, hidden), [((n_dev * share, LANES), B...  5 us
    pallas_call x1, Pallas kernels, per_device(): call(functools.partial(project, half, hidden), [((n_dev, 2, per, LANES),...  4.11 us
  transfers between devices with their start and end apart: 4, of which 4 were waited for; matrix products, arithmetic and copies ran while one was open for 0% of the time, Pallas kernels for 4%

commit v1 on v0

--- a/solution.py
+++ b/solution.py
@@ -16,22 +16,40 @@
 TN = (((0,), (0,)), ((), ()))
 VMEM = pl.BlockSpec(memory_space=pltpu.VMEM)
 SMEM = pl.BlockSpec(memory_space=pltpu.SMEM)
+HBM = pl.BlockSpec(memory_space=pltpu.HBM)
+GROUPS = 4
 
 
 def dot(a, b, dims=NN):
     return lax.dot_general(a, b, dims, preferred_element_type=F32)
 
 
-def call(body, outs, scratch, name, flops, moved):
+def call(body, ins, outs, scratch, name, flops, moved):
     return pl.pallas_call(
         body,
-        out_shape=tuple(jax.ShapeDtypeStruct(s, d) for s, d in outs),
-        out_specs=tuple(VMEM for _ in outs),
+        in_specs=list(ins),
+        out_shape=tuple(jax.ShapeDtypeStruct(s, d) for s, d, _ in outs),
+        out_specs=tuple(spec for _, _, spec in outs),
         scratch_shapes=scratch,
         name=name,
-        compiler_params=pltpu.CompilerParams(vmem_limit_bytes=24 * 2**20),
+        compiler_params=pltpu.CompilerParams(vmem_limit_bytes=20 * 2**20),
         cost_estimate=pl.CostEstimate(flops=flops, bytes_accessed=moved, transcendentals=0),
     )
+
+
+def begin(source, target, sem):
+    copy = pltpu.make_async_copy(source, target, sem)
+    copy.start()
+    return copy
+
+
+def finish_all(copies):
+    for copy in copies:
+        copy.wait()
+
+
+def span(g, size):
+    return pl.ds(g * size, size)
 
 
 def exchange(blocks):
@@ -57,12 +75,12 @@
     return jnp.concatenate([ref[p], ref[half + p]], axis=0)
 
 
-def mask_row(info, p, half, cols):
+def mask_row(length, p, half, cols):
     lane = lax.broadcasted_iota(jnp.int32, (1, LANES), 1)
     second = (lane >= cols).astype(jnp.int32)
-    row = info[0] + p + half * second
-    col = info[1] + lane - cols * second
-    return ((row < info[2]) & (col < info[2])).astype(F32)
+    row = lax.axis_index("row") * (2 * half) + p + half * second
+    col = lax.axis_index("col") * cols + lane - cols * second
+    return ((row < length[0]) & (col < length[0])).astype(F32)
 
 
 def normal(x, axis):
@@ -71,11 +89,24 @@
     return center * inverse, inverse
 
 
-def project(half, hidden, info, pair, gain, bias, lw, rw, send, nt_out, wt, gb, ls, rs):
+def project(half, hidden, length, pair_h, gain_h, bias_h, lw_h, rw_h, send, nt_out, pair, gain, bias, w, wt, gb, ls, rs, sems):
     n_dev, _, per, _ = send.shape
     cols = pair.shape[1]
-    wt[0] = flip(lw[...])
-    wt[1] = flip(rw[...])
+    step_rows = half // GROUPS
+    small = [
+        begin(lw_h, w.at[0], sems.at[0]),
+        begin(rw_h, w.at[1], sems.at[1]),
+        begin(gain_h, gain, sems.at[2]),
+        begin(bias_h, bias, sems.at[3]),
+    ]
+    tiles = []
+    for g in range(GROUPS):
+        for k in (0, 1):
+            at = pl.ds(k * half + g * step_rows, step_rows)
+            tiles.append(begin(pair_h.at[at], pair.at[at], sems.at[4 + 2 * g + k]))
+    finish_all(small)
+    wt[0] = flip(w[0])
+    wt[1] = flip(w[1])
     gb[0] = column(gain[...])
     gb[1] = column(bias[...])
 
@@ -84,14 +115,16 @@
         hat, _ = normal(x, 0)
         nt = (hat * gb[0] + gb[1]).astype(BF16)
         nt_out[:, pl.ds(pl.multiple_of(p * LANES, LANES), LANES)] = nt
-        mask = mask_row(info, p, half, cols)
+        mask = mask_row(length, p, half, cols)
         for side, scr in ((0, ls), (1, rs)):
             proj = dot(wt[side], nt)
             act = mask * jax.nn.sigmoid(proj[hidden:]) * proj[:hidden]
             scr[pl.ds(p, hidden, stride=half), :] = act
         return carry
 
-    lax.fori_loop(0, half, step, 0, unroll=2)
+    for g in range(GROUPS):
+        finish_all(tiles[2 * g : 2 * g + 2])
+        lax.fori_loop(g * step_rows, (g + 1) * step_rows, step, 0, unroll=2)
 
     def pack(d, carry):
         at = pl.ds(pl.multiple_of(d * per, per), per)
@@ -102,7 +135,7 @@
     lax.fori_loop(0, n_dev, pack, 0, unroll=4)
 
 
-def prepare(half, hidden, info, pair, cot, nt_in, lw, rw, gw, gate_out, cot_out, coef, hat_out, scale_out, wt, gwt):
+def prepare(half, hidden, length, pair, cot, nt_in, lw, rw, gw, gate_out, cot_out, coef, hat_out, scale_out, wt, gwt):
     cols = pair.shape[1]
     wt[0] = flip(lw[...])
     wt[1] = flip(rw[...])
@@ -114,10 +147,10 @@
         hat, inverse = normal(x, 0)
         hat_out[:, at] = hat
         scale_out[:, at] = jnp.broadcast_to(inverse, (8, LANES))
-        cot_out[:, at] = token_tile(cot, p, half).astype(F32).T
+        cot_out[:, at] = token_tile(cot, p, half).astype(F32).T.astype(BF16)
         nt = nt_in[:, at]
         gate_out[:, at] = jax.nn.sigmoid(dot(gwt[...], nt))
-        mask = mask_row(info, p, half, cols)
+        mask = mask_row(length, p, half, cols)
         for side in (0, 1):
             proj = dot(wt[side], nt)
             sig = jax.nn.sigmoid(proj[hidden:])
@@ -147,7 +180,7 @@
             write(r * n_col + 2 * m + 1, second)
 
 
-def multiply(n_row, n_col, half, recv, send, left, right, acc):
+def multiply(n_row, n_col, half, recv, send_h, left, right, acc, send, sems):
     def step(h, carry):
         at = pl.ds(pl.multiple_of(h * half, half), half)
         for side, out in ((0, left), (1, right)):
@@ -162,12 +195,17 @@
             send[d, at, :] = block.astype(BF16)
 
         scatter_tiles(n_row, n_col, half, acc, put)
-        return carry
-
-    lax.fori_loop(0, left.shape[0], step, 0)
-
-
-def multiply_back(n_row, n_col, half, recv, left, right, send, grad, acc):
+        begin(send.at[:, at], send_h.at[:, at], sems.at[h])
+        return carry
+
+    own = left.shape[0]
+    lax.fori_loop(0, own, step, 0)
+    for h in range(own):
+        at = span(h, half)
+        pltpu.make_async_copy(send.at[:, at], send_h.at[:, at], sems.at[h]).wait()
+
+
+def multiply_back(n_row, n_col, half, recv, left, right, send_h, grad, acc, send, sems):
     def step(h, carry):
         at = pl.ds(pl.multiple_of(h * half, half), half)
 
@@ -183,9 +221,14 @@
                 send[d, side, at, :] = block.astype(BF16)
 
             scatter_tiles(n_row, n_col, half, acc.at[side], put)
-        return carry
-
-    lax.fori_loop(0, left.shape[0], step, 0)
+        begin(send.at[:, :, at], send_h.at[:, :, at], sems.at[h])
+        return carry
+
+    own = left.shape[0]
+    lax.fori_loop(0, own, step, 0)
+    for h in range(own):
+        at = span(h, half)
+        pltpu.make_async_copy(send.at[:, :, at], send_h.at[:, :, at], sems.at[h]).wait()
 
 
 def unpack(recv, scr, side=None):
@@ -200,8 +243,14 @@
     lax.fori_loop(0, n_dev, step, 0, unroll=4)
 
 
-def middle(half, hidden, recv, gate_in, cot_in, gain, bias, ow, send, upd, og_out, gg_out, tn_out, sums, scr, owt, gb):
+def middle(half, hidden, recv, gate_h, cot_h, gain, bias, ow, send, upd_h, og_h, gg_h, tn_h, sums, gate_in, cot_in, upd, og_out, gg_out, tn_out, scr, owt, gb, sems, out_sems):
     n_dev, per, _ = send.shape
+    size = gate_in.shape[1] // GROUPS
+    fetched = []
+    for g in range(GROUPS):
+        at = span(g, size)
+        fetched.append(begin(gate_h.at[:, at], gate_in.at[:, at], sems.at[2 * g]))
+        fetched.append(begin(cot_h.at[:, at], cot_in.at[:, at], sems.at[2 * g + 1]))
     unpack(recv, scr)
     owt[...] = flip(ow[...])
     gb[0] = column(gain[...])
@@ -216,8 +265,8 @@
         tn_out[:, at] = tn
         outer = dot(owt[...], tn)
         gate = gate_in[:, at]
-        up = cot_in[:, at]
-        upd[:, at] = gate * outer
+        up = cot_in[:, at].astype(F32)
+        upd[:, at] = (gate * outer).astype(BF16)
         og = (up * gate).astype(BF16)
         og_out[:, at] = og
         gg_out[:, at] = (up * outer * gate * (1.0 - gate)).astype(BF16)
@@ -230,7 +279,15 @@
         scr[rows, :] = scale * back
         return carry
 
-    lax.fori_loop(0, half, step, 0, unroll=2)
+    stored = []
+    saved = ((upd, upd_h), (og_out, og_h), (gg_out, gg_h), (tn_out, tn_h))
+    for g in range(GROUPS):
+        finish_all(fetched[2 * g : 2 * g + 2])
+        count = half // GROUPS
+        lax.fori_loop(g * count, (g + 1) * count, step, 0, unroll=2)
+        at = span(g, size)
+        for k, (source, target) in enumerate(saved):
+            stored.append(begin(source.at[:, at], target.at[:, at], out_sems.at[4 * g + k]))
 
     def pack(d, carry):
         at = pl.ds(pl.multiple_of(d * per, per), per)
@@ -238,6 +295,7 @@
         return carry
 
     lax.fori_loop(0, n_dev, pack, 0, unroll=4)
+    finish_all(stored)
 
 
 def fold(x):
@@ -247,7 +305,7 @@
 def settle(half, upd, og, gg, tn, nt, sums, update, early, norms):
     def step(p, carry):
         at = pl.ds(pl.multiple_of(p * LANES, LANES), LANES)
-        tile = upd[:, at].T.astype(BF16)
+        tile = upd[:, at].astype(F32).T.astype(BF16)
         cols = update.shape[1]
         update[p] = tile[:cols]
         update[half + p] = tile[cols:]
@@ -260,7 +318,14 @@
     norms[1:2] = fold(sums[1])
 
 
-def finish(half, hidden, recv, coef, nt, gg, hat, lw, rw, gw, early, early_norms, parts, ng_out, scr, comb, sums):
+def finish(half, hidden, recv, coef_h, nt, gg_h, hat_h, lw, rw, gw, early, early_norms, parts, ng_h, coef, gg, hat, ng_out, scr, comb, sums, sems, out_sems):
+    size = hat.shape[1] // GROUPS
+    fetched = []
+    for g in range(GROUPS):
+        at = span(g, size)
+        fetched.append(begin(coef_h.at[:, :, at], coef.at[:, :, at], sems.at[3 * g]))
+        fetched.append(begin(gg_h.at[:, at], gg.at[:, at], sems.at[3 * g + 1]))
+        fetched.append(begin(hat_h.at[:, at], hat.at[:, at], sems.at[3 * g + 2]))
     for side in (0, 1):
         unpack(recv, scr.at[side], side)
     sums[...] = jnp.zeros_like(sums)
@@ -281,7 +346,13 @@
         sums[1] += ng
         return carry
 
-    lax.fori_loop(0, half, step, 0, unroll=2)
+    stored = []
+    for g in range(GROUPS):
+        finish_all(fetched[3 * g : 3 * g + 3])
+        count = half // GROUPS
+        lax.fori_loop(g * count, (g + 1) * count, step, 0, unroll=2)
+        at = span(g, size)
+        stored.append(begin(ng_out.at[:, at], ng_h.at[:, at], out_sems.at[g]))
     c = nt.shape[0]
     parts[...] = jnp.zeros_like(parts)
     for side in (0, 1):
@@ -295,9 +366,10 @@
     low = (exact - high.astype(F32)).astype(BF16)
     base = 5 * c + hidden
     parts[base : base + 8] = jnp.concatenate([high, low], axis=0)
-
-
-def add_up(scale, holder, device, recv, send):
+    finish_all(stored)
+
+
+def add_up(scale, holder, n_col, recv, send):
     n_dev, share, _ = recv.shape
     mine = scale * jnp.sum(recv[...].astype(F32), axis=0)
     exact = mine[0:4] + mine[4:8]
@@ -305,10 +377,25 @@
     pairs = jnp.concatenate([high, exact - high], axis=0)
     if share > 8:
         pairs = jnp.concatenate([pairs, mine[8:]], axis=0)
-    keep = (device[0] == holder).astype(F32)
+    keep = (lax.axis_index("row") * n_col + lax.axis_index("col") == holder).astype(F32)
     result = (keep * pairs + (1.0 - keep) * mine).astype(BF16)
     for d in range(n_dev):
         send[d] = result
+
+
+def deliver(totals, left, right, gating, output, norms):
+    c = left.shape[0]
+
+    def rows(k, n=c):
+        return totals[k * c : k * c + n].astype(F32)
+
+    for k, out in ((0, left), (2, right)):
+        out[:, :LANES] = rows(k)
+        out[:, LANES:] = rows(k + 1)
+    gating[...] = rows(4)
+    output[...] = rows(5)
+    exact = rows(6, 8)
+    norms[...] = exact[0:4] + exact[4:8]
 
 
 def close(half, ng, hat, scale, gain, grad_pair, gb):
@@ -353,93 +440,101 @@
     wide = half * LANES
     per = own * half
     assert 2 * cols_dev == LANES and rows_dev == 2 * half and c == LANES and hidden == LANES
-    info = jnp.stack(
-        [
-            lax.axis_index("row").astype(jnp.int32) * rows_dev,
-            lax.axis_index("col").astype(jnp.int32) * cols_dev,
-            length[0],
-        ]
-    )
     gain, bias = norm_gain[None], norm_bias[None]
     o_gain, o_bias = out_gain[None], out_bias[None]
-    vm = pltpu.VMEM
+    vm, dma = pltpu.VMEM, pltpu.SemaphoreType.DMA
     sq = (c, LANES)
+    rows = hidden * half
 
     send, nt = call(
         functools.partial(project, half, hidden),
-        [((n_dev, 2, per, LANES), BF16), ((c, wide), BF16)],
-        [vm((2, 2 * hidden, c), BF16), vm((2,) + sq, F32)] + [vm((hidden * half, LANES), F32)] * 2,
+        (SMEM,) + (HBM,) * 5,
+        [((n_dev, 2, per, LANES), BF16, VMEM), ((c, wide), BF16, VMEM)],
+        [vm(pair.shape, BF16), vm((1, c), F32), vm((1, c), F32), vm((2, c, 2 * hidden), BF16)]
+        + [vm((2, 2 * hidden, c), BF16), vm((2,) + sq, F32), vm((rows, LANES), F32)]
+        + [vm((rows, LANES), F32), dma((4 + 2 * GROUPS,))],
         "project", 300 * 10**6, 3 * 2**20,
-    )(info, pair, gain, bias, left_weight, right_weight)
+    )(length, pair, gain, bias, left_weight, right_weight)
     both = exchange(send)
     gate, cot, coef, hat, scale = call(
         functools.partial(prepare, half, hidden),
-        [((c, wide), F32), ((c, wide), F32), ((4, hidden, wide), F32), ((c, wide), F32), ((8, wide), F32)],
+        (SMEM,) + (VMEM,) * 6,
+        [((c, wide), F32, VMEM), ((c, wide), BF16, VMEM), ((4, hidden, wide), F32, VMEM)]
+        + [((c, wide), F32, VMEM), ((8, wide), F32, VMEM)],
         [vm((2, 2 * hidden, c), BF16), vm((c, c), BF16)],
         "prepare", 400 * 10**6, 9 * 2**20,
-    )(info, pair, cotangent, nt, left_weight, right_weight, gate_weight)
+    )(length, pair, cotangent, nt, left_weight, right_weight, gate_weight)
     send, left, right = call(
         functools.partial(multiply, n_row, n_col, half),
-        [((n_dev, per, LANES), BF16), ((own, tokens, tokens), BF16), ((own, tokens, tokens), BF16)],
-        [vm((tokens, tokens), F32)],
+        (VMEM,),
+        [((n_dev, per, LANES), BF16, HBM)] + [((own, tokens, tokens), BF16, VMEM)] * 2,
+        [vm((tokens, tokens), F32), vm((n_dev, per, LANES), BF16), dma((own,))],
         "multiply", 200 * 10**6, 3 * 2**20,
     )(both)
     tri = exchange(send)
     send, upd, og, gg, tn, sums = call(
         functools.partial(middle, half, hidden),
-        [((n_dev, per, LANES), BF16), ((c, wide), F32)] + [((c, wide), BF16)] * 3 + [((2,) + sq, F32)],
-        [vm((hidden * half, LANES), F32), vm((c, hidden), BF16), vm((2,) + sq, F32)],
+        (VMEM, HBM, HBM, VMEM, VMEM, VMEM),
+        [((n_dev, per, LANES), BF16, VMEM)] + [((c, wide), BF16, HBM)] * 4 + [((2,) + sq, F32, VMEM)],
+        [vm((c, wide), F32)] + [vm((c, wide), BF16)] * 5 + [vm((rows, LANES), F32)]
+        + [vm((c, hidden), BF16), vm((2,) + sq, F32), dma((2 * GROUPS,)), dma((4 * GROUPS,))],
         "middle", 200 * 10**6, 6 * 2**20,
     )(tri, gate, cot, o_gain, o_bias, out_weight)
     grad = exchange(send)
     update, early, early_norms = call(
         functools.partial(settle, half),
-        [((rows_dev, cols_dev, c), BF16), ((2,) + sq, F32), ((8, LANES), F32)],
+        (VMEM,) * 6,
+        [((rows_dev, cols_dev, c), BF16, VMEM), ((2,) + sq, F32, VMEM), ((8, LANES), F32, VMEM)],
         [],
         "settle", 200 * 10**6, 4 * 2**20,
     )(upd, og, gg, tn, nt, sums)
     (send,) = call(
         functools.partial(multiply_back, n_row, n_col, half),
-        [((n_dev, 2, per, LANES), BF16)],
-        [vm((tokens, tokens), BF16), vm((2, tokens, tokens), F32)],
+        (VMEM,) * 3,
+        [((n_dev, 2, per, LANES), BF16, HBM)],
+        [vm((tokens, tokens), BF16), vm((2, tokens, tokens), F32)]
+        + [vm((n_dev, 2, per, LANES), BF16), dma((own,))],
         "multiply_back", 300 * 10**6, 3 * 2**20,
     )(grad, left, right)
     back = exchange(send)
-    used = 5 * c + hidden + 8
-    assert (5 * c + hidden) % 8 == 0
-    share = -(-used // (n_dev * 8)) * 8
-    while (5 * c + hidden) % share:
+    base = 5 * c + hidden
+    assert base % 8 == 0
+    share = -(-(base + 8) // (n_dev * 8)) * 8
+    while base % share:
         share += 8
-    device = (lax.axis_index("row") * n_col + lax.axis_index("col")).astype(jnp.int32)[None]
     parts, ng = call(
         functools.partial(finish, half, hidden),
-        [((n_dev * share, LANES), BF16), ((c, wide), F32)],
-        [vm((2, hidden * half, LANES), F32), vm((2, 2 * hidden, wide), BF16), vm((2,) + sq, F32)],
+        (VMEM, HBM, VMEM, HBM, HBM) + (VMEM,) * 5,
+        [((n_dev * share, LANES), BF16, VMEM), ((c, wide), F32, HBM)],
+        [vm((4, hidden, wide), F32), vm((c, wide), BF16), vm((c, wide), F32), vm((c, wide), F32)]
+        + [vm((2, rows, LANES), F32), vm((2, 2 * hidden, wide), BF16), vm((2,) + sq, F32)]
+        + [dma((3 * GROUPS,)), dma((GROUPS,))],
         "finish", 500 * 10**6, 10 * 2**20,
     )(back, coef, nt, gg, hat, left_weight, right_weight, gate_weight, early, early_norms)
     (send,) = call(
-        functools.partial(add_up, 1.0 / tokens, (5 * c + hidden) // share),
-        [((n_dev, share, LANES), BF16)],
+        functools.partial(add_up, 1.0 / tokens, base // share, n_col),
+        (VMEM,),
+        [((n_dev, share, LANES), BF16, VMEM)],
         [],
         "add_up", 10**6, 2**19,
-    )(device, exchange(parts.reshape(n_dev, share, LANES)))
-    totals = exchange(send).reshape(n_dev * share, LANES).astype(F32)
+    )(exchange(parts.reshape(n_dev, share, LANES)))
+    totals = exchange(send).reshape(n_dev * share, LANES)
     (grad_pair,) = call(
         functools.partial(close, half),
-        [((rows_dev, cols_dev, c), BF16)],
+        (VMEM,) * 4,
+        [((rows_dev, cols_dev, c), BF16, VMEM)],
         [vm(sq, F32)],
         "close", 50 * 10**6, 3 * 2**20,
     )(ng, hat, scale, gain)
-    base = 5 * c + hidden
-    return (
-        update,
-        grad_pair,
-        jnp.concatenate([totals[:c], totals[c : 2 * c]], axis=1),
-        jnp.concatenate([totals[2 * c : 3 * c], totals[3 * c : 4 * c]], axis=1),
-        totals[4 * c : 5 * c],
-        totals[5 * c : base],
-        totals[base : base + 4] + totals[base + 4 : base + 8],
-    )
+    grads = call(
+        deliver,
+        (VMEM,),
+        [((c, 2 * hidden), F32, VMEM)] * 2
+        + [((c, c), F32, VMEM), ((hidden, c), F32, VMEM), ((4, c), F32, VMEM)],
+        [],
+        "deliver", 10**6, 2**20,
+    )(totals)
+    return (update, grad_pair) + tuple(grads)
 
 
 def solution(mesh):

time: 161 us -> 162 us (level)
  blocking collectives: 50.3 us -> 64.8 us
  waiting for transfers between devices: 42.8 us -> 33 us
  starting transfers between devices: 15.9 us -> 11.4 us
  Pallas kernels: 23.3 us -> 26.5 us
    all_to_all x2 -> x3, blocking collectives: 50.3 us -> 64.8 us  [exchange(): return lax.all_to_all(blocks, BOTH, split_axis=0, concat_axis=0, tiled=True)]
    all_to_all x4 -> x3, waiting for transfers between devices: 42.8 us -> 33 us  [exchange(): return lax.all_to_all(blocks, BOTH, split_axis=0, concat_axis=0, tiled=True)]
    all_to_all x4 -> x3, starting transfers between devices: 15.9 us -> 11.4 us  [exchange(): return lax.all_to_all(blocks, BOTH, split_axis=0, concat_axis=0, tiled=True)]
    pallas_call x9 -> x10, Pallas kernels: 23.3 us -> 26.5 us  [the longest x1 5.69 us: per_device(): call(functools.partial(finish, half, hidden), (VMEM, HBM, VMEM, HBM, HBM)...]
  transfers between devices with their start and end apart: 4 -> 3, of which waited for: 4 -> 3; matrix products, arithmetic and copies ran while one was open for 0% -> 0% of each run, Pallas kernels for 4% -> 4%
where the time goes in v1:
time: 162 us; the launch traced here: 161 us
  blocking collectives  64.8 us (40%)
  waiting for transfers between devices  33 us (20%)
  Pallas kernels  26.5 us (16%)
  local copies, waits for them, and re-layouts  23.8 us (15%)
  starting transfers between devices  11.4 us (7%)
    all_to_all x3, blocking collectives, exchange(): return lax.all_to_all(blocks, BOTH, split_axis=0, concat_axis=0, tiled=True)  64.8 us
    all_to_all x3, waiting for transfers between devices, exchange(): return lax.all_to_all(blocks, BOTH, split_axis=0, concat_axis=0, tiled=True)  33 us
    unnamed x66, local copies, waits for them, and re-layouts  23.8 us
    all_to_all x3, starting transfers between devices, exchange(): return lax.all_to_all(blocks, BOTH, split_axis=0, concat_axis=0, tiled=True)  11.4 us
    pallas_call x1, Pallas kernels, per_device(): call(functools.partial(finish, half, hidden), (VMEM, HBM, VMEM, HBM, HBM)...  5.69 us
    pallas_call x1, Pallas kernels, per_device(): call(functools.partial(project, half, hidden), (SMEM,) + (HBM,) * 5, [((n...  5.03 us
    pallas_call x1, Pallas kernels, per_device(): call(functools.partial(middle, half, hidden), (VMEM, HBM, HBM, VMEM, VMEM...  3.88 us
  transfers between devices with their start and end apart: 3, of which 3 were waited for; matrix products, arithmetic and copies ran while one was open for 0% of the time, Pallas kernels for 4%

profile of v1, /device:TPU:0, one launch (start us, length us, event | category | flops | bytes accessed | tf_op | source)
XLA Modules:
  0.0 161.1 jit_solution(3073337978113161255)
XLA Ops:
  1.3 0.0 copy-start.9
  1.3 1.0 copy-done.9
  2.4 0.8 copy-done.20
  3.2 0.8 copy-done.22
  4.0 0.7 copy-done.28
  4.7 0.7 copy-done.32
  5.4 5.0 %project.1 = (bf16[32,2,64,128]{3,2,1,0:T(8,128)(2,1)S(1)}, bf16[128,2048]{1,0:T(8,128)(2,1)S(1)}) custom-call(s32[1]{0:T(128)S(6)} %copy.18.length, bf16[32,64,128]{2,1,0:T(8,128)(2,1)S(1)} %copy-done.9, f32[1,128]{1,0:T(1,128)S(1)} %bitcast.8, f32[1,128]{1,0:T(1,128)S(1)} %bitcast.12, bf16[128,256]{1,0:T(8,128)(2,1)S(1)} %copy-done.20, ...), custom_call_target="tpu_custom_call" | custom-call | flops 300000000 | bytes 3145728 | tf_op jit(solution)/shard_map/project/pallas_call | solution.py:449
  10.4 32.1 %all_to_all.30.recv = bf16[32,2,64,128]{3,2,1,0:T(8,128)(2,1)S(1)} all-to-all(bf16[32,2,64,128]{3,2,1,0:T(8,128)(2,1)S(1)} %get-tuple-element.33), channel_id=1, replica_groups=mesh['row'=8,'col'=4] {'row','col'}, dimensions={0} | all-to-all | bytes 2097152 | tf_op jit(solution)/shard_map/all_to_all | solution.py:56
  42.5 2.2 %multiply.1 = (bf16[32,64,128]{2,1,0:T(8,128)(2,1)}, bf16[4,256,256]{2,1,0:T(8,128)(2,1)S(1)}, bf16[4,256,256]{2,1,0:T(8,128)(2,1)S(1)}) custom-call(bf16[32,2,64,128]{3,2,1,0:T(8,128)(2,1)S(1)} %all_to_all.30.recv), custom_call_target="tpu_custom_call" | custom-call | flops 200000000 | bytes 3145728 | tf_op jit(solution)/shard_map/multiply/pallas_call | solution.py:467
  44.7 0.8 copy-done.7
  45.5 4.6 %all-to-all-start.1 = ((bf16[32,64,128]{2,1,0:T(8,128)(2,1)}), bf16[32,64,128]{2,1,0:T(8,128)(2,1)S(1)}, u32[]{:S(2)}, u32[]{:S(2)}) async-start(bf16[32,64,128]{2,1,0:T(8,128)(2,1)} %get-tuple-element.34), calls=%async_computation.1 | async-start | bytes 1048576 | tf_op jit(solution)/shard_map/all_to_all | solution.py:56
  50.1 0.0 copy-start.11
  50.1 1.0 copy-done.11
  51.2 2.5 %prepare.1 = (f32[128,2048]{1,0:T(8,128)S(1)}, bf16[128,2048]{1,0:T(8,128)(2,1)S(1)}, f32[4,128,2048]{2,1,0:T(8,128)S(1)}, f32[128,2048]{1,0:T(8,128)S(1)}, f32[8,2048]{1,0:T(8,128)S(1)}) custom-call(s32[1]{0:T(128)S(6)} %copy.18.length, bf16[32,64,128]{2,1,0:T(8,128)(2,1)S(1)} %copy-done.10, bf16[32,64,128]{2,1,0:T(8,128)(2,1)S(1)} %copy-done.11, ...), custom_call_target="tpu_custom_call" | custom-call | flops 400000000 | bytes 9437184 | tf_op jit(solution)/shard_map/prepare/pallas_call | solution.py:459
  53.7 2.0 %copy-done = f32[4,128,2048]{2,1,0:T(8,128)} copy-done((f32[4,128,2048]{2,1,0:T(8,128)}, f32[4,128,2048]{2,1,0:T(8,128)S(1)}, u32[]{:S(2)}) %copy-start) | copy-done | bytes 4194328
  55.7 1.0 copy-done.5
  56.6 0.8 copy-done.18
  57.4 6.9 %all-to-all-done.1.recv = bf16[32,64,128]{2,1,0:T(8,128)(2,1)S(1)} async-done(((bf16[32,64,128]{2,1,0:T(8,128)(2,1)}), bf16[32,64,128]{2,1,0:T(8,128)(2,1)S(1)}, u32[]{:S(2)}, u32[]{:S(2)}) %all-to-all-start.1) | async-done | bytes 524320 | tf_op jit(solution)/shard_map/all_to_all | solution.py:56
  64.3 0.0 copy-done.30
  64.3 1.2 copy-done.6
  65.6 1.0 copy-done.19
  66.6 3.9 %middle.1 = (bf16[32,64,128]{2,1,0:T(8,128)(2,1)S(1)}, bf16[128,2048]{1,0:T(8,128)(2,1)S(1)}, bf16[128,2048]{1,0:T(8,128)(2,1)S(1)}, bf16[128,2048]{1,0:T(8,128)...) custom-call(bf16[32,64,128]{2,1,0:T(8,128)(2,1)S(1)} %all-to-all-done.1.recv, ...), custom_call_target="tpu_custom_call" | custom-call | flops 200000000 | bytes 6291456 | tf_op jit(solution)/shard_map/middle/pallas_call | solution.py:475
  70.5 0.8 copy-done.16
  71.3 0.7 copy-done.25
  72.0 18.2 %all_to_all.31.recv = bf16[32,64,128]{2,1,0:T(8,128)(2,1)S(1)} all-to-all(bf16[32,64,128]{2,1,0:T(8,128)(2,1)S(1)} %get-tuple-element.44), channel_id=1, replica_groups=mesh['row'=8,'col'=4] {'row','col'}, dimensions={0} | all-to-all | bytes 1048576 | tf_op jit(solution)/shard_map/all_to_all | solution.py:56
  90.2 0.0 copy-done.14
  90.2 1.0 copy-done.8
  91.2 1.8 %multiply_back.1 = bf16[32,2,64,128]{3,2,1,0:T(8,128)(2,1)S(1)} custom-call(bf16[32,64,128]{2,1,0:T(8,128)(2,1)S(1)} %all_to_all.31.recv, bf16[4,256,256]{2,1,0:T(8,128)(2,1)S(1)} %get-tuple-element.45.left, bf16[4,256,256]{2,1,0:T(8,128)(2,1)S(1)} %copy-done.8), custom_call_target="tpu_custom_call" | custom-call | flops 300000000 | bytes 3145728 | tf_op jit(solution)/shard_map/multiply_back/pallas_call | solution.py:491
  93.1 1.0 copy-done.2
  94.1 4.2 %all-to-all-start.3 = ((bf16[32,2,64,128]{3,2,1,0:T(8,128)(2,1)}), bf16[32,2,64,128]{3,2,1,0:T(8,128)(2,1)S(1)}, u32[]{:S(2)}, u32[]{:S(2)}) async-start(bf16[32,2,64,128]{3,2,1,0:T(8,128)(2,1)} %copy-done.2), calls=%async_computation.3 | async-start | bytes 2097152 | tf_op jit(solution)/shard_map/all_to_all | solution.py:56
  98.2 0.0 copy-start.13
  98.3 1.0 copy-done.13
  99.3 1.0 copy-done.15
  100.3 1.0 copy-done.17
  101.4 0.9 copy-done.26
  102.3 1.6 %settle.1 = (bf16[32,64,128]{2,1,0:T(8,128)(2,1)}, f32[2,128,128]{2,1,0:T(8,128)S(1)}, f32[8,128]{1,0:T(8,128)S(1)}) custom-call(bf16[128,2048]{1,0:T(8,128)(2,1)S(1)} %copy-done.13, bf16[128,2048]{1,0:T(8,128)(2,1)S(1)} %copy-done.15, bf16[128,2048]{1,0:T(8,128)(2,1)S(1)} %get-tuple-element.40.gg.gg_h, bf16[128,2048]{1,0:T(8,128)(2,1)S(1)} %copy-done.17, ...), custom_call_target="tpu_custom_call" | custom-call | flops 200000000 | bytes 4194304 | tf_op jit(solution)/shard_map/settle/pallas_call | solution.py:484
  103.9 19.2 %all-to-all-done.3.recv = bf16[32,2,64,128]{3,2,1,0:T(8,128)(2,1)S(1)} async-done(((bf16[32,2,64,128]{3,2,1,0:T(8,128)(2,1)}), bf16[32,2,64,128]{3,2,1,0:T(8,128)(2,1)S(1)}, u32[]{:S(2)}, u32[]{:S(2)}) %all-to-all-start.3) | async-done | bytes 1048608 | tf_op jit(solution)/shard_map/all_to_all | solution.py:56
  123.2 2.2 %copy-done.1 = f32[4,128,2048]{2,1,0:T(8,128)S(1)} copy-done((f32[4,128,2048]{2,1,0:T(8,128)S(1)}, f32[4,128,2048]{2,1,0:T(8,128)}, u32[]{:S(2)}) %copy-start.1) | copy-done | bytes 4194328
  125.4 5.7 %finish.1 = (bf16[1024,128]{1,0:T(8,128)(2,1)S(1)}, f32[128,2048]{1,0:T(8,128)S(1)}) custom-call(bf16[32,2,64,128]{3,2,1,0:T(8,128)(2,1)S(1)} %all-to-all-done.3.recv, f32[4,128,2048]{2,1,0:T(8,128)S(1)} %copy-done.1, bf16[128,2048]{1,0:T(8,128)(2,1)S(1)} %get-tuple-element.35.nt_in.nt, bf16[128,2048]{1,0:T(8,128)(2,1)S(1)} %get-tuple-element.40.gg.gg_h, ...), custom_call_target="tpu_custom_call" | custom-call | flops 500000000 | bytes 10485760 | tf_op jit(solution)/shard_map/finish/pallas_call | solution.py:505
  131.1 1.0 copy-done.3
  132.1 14.6 %all_to_all.32.recv = bf16[32,32,128]{2,1,0:T(8,128)(2,1)S(1)} all-to-all(bf16[32,32,128]{2,1,0:T(8,128)(2,1)S(1)} %bitcast.7), channel_id=1, replica_groups=mesh['row'=8,'col'=4] {'row','col'}, dimensions={0} | all-to-all | bytes 524288 | tf_op jit(solution)/shard_map/all_to_all | solution.py:56
  146.6 0.8 add_up.1
  147.4 2.7 %all-to-all-start.5 = ((bf16[32,32,128]{2,1,0:T(8,128)(2,1)}), bf16[32,32,128]{2,1,0:T(8,128)(2,1)S(1)}, u32[]{:S(2)}, u32[]{:S(2)}) async-start(bf16[32,32,128]{2,1,0:T(8,128)(2,1)} %add_up.1), calls=%async_computation.5 | async-start | bytes 524288 | tf_op jit(solution)/shard_map/all_to_all | solution.py:56
  150.1 0.0 copy-done.29
  150.1 1.2 copy-done.4
  151.3 2.1 %close.1 = bf16[32,64,128]{2,1,0:T(8,128)(2,1)} custom-call(f32[128,2048]{1,0:T(8,128)S(1)} %copy-done.4, f32[128,2048]{1,0:T(8,128)S(1)} %get-tuple-element.48.hat_h.hat, f32[8,2048]{1,0:T(8,128)S(1)} %get-tuple-element.52.scale, f32[1,128]{1,0:T(1,128)S(1)} %bitcast.9), custom_call_target="tpu_custom_call" | custom-call | flops 50000000 | bytes 3145728 | tf_op jit(solution)/shard_map/close/pallas_call | solution.py:522
  153.4 6.9 %all-to-all-done.5 = bf16[32,32,128]{2,1,0:T(8,128)(2,1)S(1)} async-done(((bf16[32,32,128]{2,1,0:T(8,128)(2,1)}), bf16[32,32,128]{2,1,0:T(8,128)(2,1)S(1)}, u32[]{:S(2)}, u32[]{:S(2)}) %all-to-all-start.5) | async-done | bytes 262176 | tf_op jit(solution)/shard_map/all_to_all | solution.py:56
  160.3 0.8 deliver.1
  (37 shorter events, 0.1 us)
Async XLA Ops:
  0.6 63.7 %copy-start.31 = (f32[128]{0:T(128)S(1)}, f32[128]{0:T(128)}, u32[]{:S(2)}) copy-start(f32[128]{0:T(128)} %param.20) | copy-start | bytes 1540
  0.6 63.7 %copy-start.30 = (f32[128]{0:T(128)S(1)}, f32[128]{0:T(128)}, u32[]{:S(2)}) copy-start(f32[128]{0:T(128)} %param.19) | copy-start | bytes 1540
  1.3 1.0 copy-start.9
  2.4 0.8 copy-start.20
  3.2 0.8 copy-start.22
  4.0 0.7 copy-start.28
  4.7 0.7 copy-start.32
  5.4 44.7 %copy-start.10 = (bf16[32,64,128]{2,1,0:T(8,128)(2,1)S(1)}, bf16[32,64,128]{2,1,0:T(8,128)(2,1)}, u32[]{:S(2)}) copy-start(bf16[32,64,128]{2,1,0:T(8,128)(2,1)} %pair.1) | copy-start | bytes 1572868
  5.4 44.7 %copy-start.21 = (bf16[128,256]{1,0:T(8,128)(2,1)S(1)}, bf16[128,256]{1,0:T(8,128)(2,1)}, u32[]{:S(2)}) copy-start(bf16[128,256]{1,0:T(8,128)(2,1)} %lw.3) | copy-start | bytes 196612
  5.4 44.7 %copy-start.23 = (bf16[128,256]{1,0:T(8,128)(2,1)S(1)}, bf16[128,256]{1,0:T(8,128)(2,1)}, u32[]{:S(2)}) copy-start(bf16[128,256]{1,0:T(8,128)(2,1)} %rw.3) | copy-start | bytes 196612
  5.4 44.8 %copy-start.24 = (bf16[128,128]{1,0:T(8,128)(2,1)S(1)}, bf16[128,128]{1,0:T(8,128)(2,1)}, u32[]{:S(2)}) copy-start(bf16[128,128]{1,0:T(8,128)(2,1)} %gw.3) | copy-start | bytes 98308
  5.4 59.0 %copy-start.27 = (bf16[128,128]{1,0:T(8,128)(2,1)S(1)}, bf16[128,128]{1,0:T(8,128)(2,1)}, u32[]{:S(2)}) copy-start(bf16[128,128]{1,0:T(8,128)(2,1)} %ow.1) | copy-start | bytes 98308
  44.7 0.8 copy-start.7
  45.5 18.8 %all-to-all-start.1 = ((bf16[32,64,128]{2,1,0:T(8,128)(2,1)}), bf16[32,64,128]{2,1,0:T(8,128)(2,1)S(1)}, u32[]{:S(2)}, u32[]{:S(2)}) async-start(bf16[32,64,128]{2,1,0:T(8,128)(2,1)} %get-tuple-element.34), calls=%async_computation.1 | async-start | bytes 1048576 | tf_op jit(solution)/shard_map/all_to_all | solution.py:56
  50.1 1.0 copy-start.11
  53.7 2.0 %copy-start = (f32[4,128,2048]{2,1,0:T(8,128)}, f32[4,128,2048]{2,1,0:T(8,128)S(1)}, u32[]{:S(2)}) copy-start(f32[4,128,2048]{2,1,0:T(8,128)S(1)} %get-tuple-element.47.coef_h) | copy-start | bytes 12582916
  55.6 1.0 copy-start.5
  56.6 0.8 copy-start.18
  64.3 1.2 copy-start.6
  65.6 1.0 copy-start.19
  70.5 0.8 copy-start.16
  71.3 0.7 copy-start.25
  71.9 18.2 %copy-start.12 = (bf16[128,2048]{1,0:T(8,128)(2,1)}, bf16[128,2048]{1,0:T(8,128)(2,1)S(1)}, u32[]{:S(2)}) copy-start(bf16[128,2048]{1,0:T(8,128)(2,1)S(1)} %get-tuple-element.38.upd) | copy-start | bytes 1572868
  72.0 18.2 %copy-start.14 = (bf16[128,2048]{1,0:T(8,128)(2,1)}, bf16[128,2048]{1,0:T(8,128)(2,1)S(1)}, u32[]{:S(2)}) copy-start(bf16[128,2048]{1,0:T(8,128)(2,1)S(1)} %get-tuple-element.39.og) | copy-start | bytes 1572868
  90.2 1.0 copy-start.8
  93.1 1.0 copy-start.2
  94.1 29.1 %all-to-all-start.3 = ((bf16[32,2,64,128]{3,2,1,0:T(8,128)(2,1)}), bf16[32,2,64,128]{3,2,1,0:T(8,128)(2,1)S(1)}, u32[]{:S(2)}, u32[]{:S(2)}) async-start(bf16[32,2,64,128]{3,2,1,0:T(8,128)(2,1)} %copy-done.2), calls=%async_computation.3 | async-start | bytes 2097152 | tf_op jit(solution)/shard_map/all_to_all | solution.py:56
  98.2 1.0 copy-start.13
  99.3 1.0 copy-start.15
  100.3 1.0 copy-start.17
  101.4 0.9 copy-start.26
  123.2 2.2 %copy-start.1 = (f32[4,128,2048]{2,1,0:T(8,128)S(1)}, f32[4,128,2048]{2,1,0:T(8,128)}, u32[]{:S(2)}) copy-start(f32[4,128,2048]{2,1,0:T(8,128)} %copy-done) | copy-start | bytes 12582916
  125.4 24.7 %copy-start.29 = (f32[128]{0:T(128)S(1)}, f32[128]{0:T(128)}, u32[]{:S(2)}) copy-start(f32[128]{0:T(128)} %param.14) | copy-start | bytes 1540
  131.1 1.0 copy-start.3
  147.4 12.9 %all-to-all-start.5 = ((bf16[32,32,128]{2,1,0:T(8,128)(2,1)}), bf16[32,32,128]{2,1,0:T(8,128)(2,1)S(1)}, u32[]{:S(2)}, u32[]{:S(2)}) async-start(bf16[32,32,128]{2,1,0:T(8,128)(2,1)} %add_up.1), calls=%async_computation.5 | async-start | bytes 524288 | tf_op jit(solution)/shard_map/all_to_all | solution.py:56
  150.1 1.2 copy-start.4

commit v2 on v1

--- a/solution.py
+++ b/solution.py
@@ -25,16 +25,28 @@
 
 
 def call(body, ins, outs, scratch, name, flops, moved):
-    return pl.pallas_call(
+    run = pl.pallas_call(
         body,
         in_specs=list(ins),
-        out_shape=tuple(jax.ShapeDtypeStruct(s, d) for s, d, _ in outs),
+        out_shape=tuple(
+            pltpu.HBM(s, d) if spec is HBM else jax.ShapeDtypeStruct(s, d) for s, d, spec in outs
+        ),
         out_specs=tuple(spec for _, _, spec in outs),
         scratch_shapes=scratch,
         name=name,
         compiler_params=pltpu.CompilerParams(vmem_limit_bytes=20 * 2**20),
         cost_estimate=pl.CostEstimate(flops=flops, bytes_accessed=moved, transcendentals=0),
     )
+
+    def placed(*args):
+        return run(
+            *[
+                pltpu.with_memory_space_constraint(x, pltpu.HBM) if spec is HBM else x
+                for x, spec in zip(args, ins, strict=True)
+            ]
+        )
+
+    return placed
 
 
 def begin(source, target, sem):

time: 162 us -> 150 us (0.926)
  local copies, waits for them, and re-layouts: 23.8 us -> 9.02 us
    unnamed x66 -> x42, local copies, waits for them, and re-layouts: 23.8 us -> 9.02 us
where the time goes in v2:
time: 150 us; the launch traced here: 149 us
  blocking collectives  64.9 us (43%)
  waiting for transfers between devices  34 us (23%)
  Pallas kernels  28.1 us (19%)
  starting transfers between devices  11.4 us (8%)
  local copies, waits for them, and re-layouts  9.02 us (6%)
  between operations  1.65 us (1%)
    all_to_all x3, blocking collectives, exchange(): return lax.all_to_all(blocks, BOTH, split_axis=0, concat_axis=0, tiled=True)  64.9 us
    all_to_all x3, waiting for transfers between devices, exchange(): return lax.all_to_all(blocks, BOTH, split_axis=0, concat_axis=0, tiled=True)  34 us
    pallas_call x10, Pallas kernels, placed(): run(*[pltpu.with_memory_space_constraint(x, pltpu.HBM) if spec is HBM els...  28.1 us
    all_to_all x3, starting transfers between devices, exchange(): return lax.all_to_all(blocks, BOTH, split_axis=0, concat_axis=0, tiled=True)  11.4 us
    unnamed x42, local copies, waits for them, and re-layouts  9.02 us
  transfers between devices with their start and end apart: 3, of which 3 were waited for; matrix products, arithmetic and copies ran while one was open for 0% of the time, Pallas kernels for 4%

profile of v2, /device:TPU:0, one launch (start us, length us, event | category | flops | bytes accessed | tf_op | source)
XLA Modules:
  0.0 149.0 jit_solution(269703040865547706)
XLA Ops:
  0.6 0.0 copy-start.13
  0.6 0.0 copy-start.12
  0.7 0.0 copy-start.6
  0.7 0.0 copy-start.14
  0.7 0.0 copy-start.7
  0.7 0.0 copy-start.17
  0.7 0.0 copy-start.20
  0.7 0.0 copy-start.19
  1.4 5.0 %project.1 = (bf16[32,2,64,128]{3,2,1,0:T(8,128)(2,1)S(1)}, bf16[128,2048]{1,0:T(8,128)(2,1)S(1)}) custom-call(s32[1]{0:T(128)S(6)} %copy.18.length, bf16[32,64,128]{2,1,0:T(8,128)(2,1)} %pair.1, f32[1,128]{1,0:T(1,128)} %bitcast.8, f32[1,128]{1,0:T(1,128)} %bitcast.12, bf16[128,256]{1,0:T(8,128)(2,1)} %lw.3, bf16[128,256]{1,0:T(8,128)(2,1)} %rw.3), custom_call_target="tpu_custom_call" | custom-call | flops 300000000 | bytes 3145728 | tf_op jit(solution)/shard_map/project/pallas_call | solution.py:42
  6.5 32.1 %all_to_all.30.recv = bf16[32,2,64,128]{3,2,1,0:T(8,128)(2,1)S(1)} all-to-all(bf16[32,2,64,128]{3,2,1,0:T(8,128)(2,1)S(1)} %get-tuple-element.33), channel_id=1, replica_groups=mesh['row'=8,'col'=4] {'row','col'}, dimensions={0} | all-to-all | bytes 2097152 | tf_op jit(solution)/shard_map/all_to_all | solution.py:68
  38.6 2.2 %multiply.1 = (bf16[32,64,128]{2,1,0:T(8,128)(2,1)}, bf16[4,256,256]{2,1,0:T(8,128)(2,1)S(1)}, bf16[4,256,256]{2,1,0:T(8,128)(2,1)S(1)}) custom-call(bf16[32,2,64,128]{3,2,1,0:T(8,128)(2,1)S(1)} %all_to_all.30.recv), custom_call_target="tpu_custom_call" | custom-call | flops 200000000 | bytes 3145728 | tf_op jit(solution)/shard_map/multiply/pallas_call | solution.py:42
  40.8 4.6 %all-to-all-start.1 = ((bf16[32,64,128]{2,1,0:T(8,128)(2,1)}), bf16[32,64,128]{2,1,0:T(8,128)(2,1)S(1)}, u32[]{:S(2)}, u32[]{:S(2)}) async-start(bf16[32,64,128]{2,1,0:T(8,128)(2,1)} %get-tuple-element.34), calls=%async_computation.1 | async-start | bytes 1048576 | tf_op jit(solution)/shard_map/all_to_all | solution.py:68
  45.4 0.0 copy-done.13
  45.4 0.0 copy-done.12
  45.4 0.0 copy-done.6
  45.4 0.0 copy-done.14
  45.4 0.0 copy-done.7
  45.4 2.6 %prepare.1 = (f32[128,2048]{1,0:T(8,128)S(1)}, bf16[128,2048]{1,0:T(8,128)(2,1)S(1)}, f32[4,128,2048]{2,1,0:T(8,128)S(1)}, f32[128,2048]{1,0:T(8,128)S(1)}, f32[8,2048]{1,0:T(8,128)S(1)}) custom-call(s32[1]{0:T(128)S(6)} %copy.18.length, bf16[32,64,128]{2,1,0:T(8,128)(2,1)S(1)} %copy-done.6, bf16[32,64,128]{2,1,0:T(8,128)(2,1)S(1)} %copy-done.7, ...), custom_call_target="tpu_custom_call" | custom-call | flops 400000000 | bytes 9437184 | tf_op jit(solution)/shard_map/prepare/pallas_call | solution.py:42
  48.0 0.0 copy-start
  48.0 1.9 %copy-done = f32[4,128,2048]{2,1,0:T(8,128)} copy-done((f32[4,128,2048]{2,1,0:T(8,128)}, f32[4,128,2048]{2,1,0:T(8,128)S(1)}, u32[]{:S(2)}) %copy-start) | copy-done | bytes 4194328
  49.9 1.0 copy-done.1
  51.0 1.0 copy-done.5
  52.0 0.8 copy-done.11
  52.8 6.9 %all-to-all-done.1.recv = bf16[32,64,128]{2,1,0:T(8,128)(2,1)S(1)} async-done(((bf16[32,64,128]{2,1,0:T(8,128)(2,1)}), bf16[32,64,128]{2,1,0:T(8,128)(2,1)S(1)}, u32[]{:S(2)}, u32[]{:S(2)}) %all-to-all-start.1) | async-done | bytes 524320 | tf_op jit(solution)/shard_map/all_to_all | solution.py:68
  59.6 0.0 copy-done.17
  59.6 0.0 copy-done.19
  59.6 4.8 %middle.1 = (bf16[32,64,128]{2,1,0:T(8,128)(2,1)S(1)}, bf16[128,2048]{1,0:T(8,128)(2,1)}, bf16[128,2048]{1,0:T(8,128)(2,1)}, bf16[128,2048]{1,0:T(8,128)(2,1)}, ...) custom-call(bf16[32,64,128]{2,1,0:T(8,128)(2,1)S(1)} %all-to-all-done.1.recv, f32[128,2048]{1,0:T(8,128)} %copy-done.5, ...), custom_call_target="tpu_custom_call" | custom-call | flops 200000000 | bytes 6291456 | tf_op jit(solution)/shard_map/middle/pallas_call | solution.py:42
  64.5 0.0 copy-start.15
  64.5 0.0 copy-start.8
  64.5 18.2 %all_to_all.31.recv = bf16[32,64,128]{2,1,0:T(8,128)(2,1)S(1)} all-to-all(bf16[32,64,128]{2,1,0:T(8,128)(2,1)S(1)} %get-tuple-element.44), channel_id=1, replica_groups=mesh['row'=8,'col'=4] {'row','col'}, dimensions={0} | all-to-all | bytes 1048576 | tf_op jit(solution)/shard_map/all_to_all | solution.py:68
  82.7 2.4 %multiply_back.1 = bf16[32,2,64,128]{3,2,1,0:T(8,128)(2,1)} custom-call(bf16[32,64,128]{2,1,0:T(8,128)(2,1)S(1)} %all_to_all.31.recv, bf16[4,256,256]{2,1,0:T(8,128)(2,1)S(1)} %get-tuple-element.45.left, bf16[4,256,256]{2,1,0:T(8,128)(2,1)S(1)} %get-tuple-element.46.right), custom_call_target="tpu_custom_call" | custom-call | flops 300000000 | bytes 3145728 | tf_op jit(solution)/shard_map/multiply_back/pallas_call | solution.py:42
  85.2 4.2 %all-to-all-start.3 = ((bf16[32,2,64,128]{3,2,1,0:T(8,128)(2,1)}), bf16[32,2,64,128]{3,2,1,0:T(8,128)(2,1)S(1)}, u32[]{:S(2)}, u32[]{:S(2)}) async-start(bf16[32,2,64,128]{3,2,1,0:T(8,128)(2,1)} %multiply_back.1), calls=%async_computation.3 | async-start | bytes 2097152 | tf_op jit(solution)/shard_map/all_to_all | solution.py:68
  89.4 1.0 copy-done.9
  90.4 1.0 copy-done.10
  91.5 0.9 copy-done.16
  92.4 1.6 %settle.1 = (bf16[32,64,128]{2,1,0:T(8,128)(2,1)}, f32[2,128,128]{2,1,0:T(8,128)S(1)}, f32[8,128]{1,0:T(8,128)S(1)}) custom-call(bf16[128,2048]{1,0:T(8,128)(2,1)S(1)} %copy-done.8, bf16[128,2048]{1,0:T(8,128)(2,1)S(1)} %copy-done.9, bf16[128,2048]{1,0:T(8,128)(2,1)S(1)} %copy-done.3, bf16[128,2048]{1,0:T(8,128)(2,1)S(1)} %copy-done.10, ...), custom_call_target="tpu_custom_call" | custom-call | flops 200000000 | bytes 4194304 | tf_op jit(solution)/shard_map/settle/pallas_call | solution.py:42
  94.0 20.3 %all-to-all-done.3.recv = bf16[32,2,64,128]{3,2,1,0:T(8,128)(2,1)S(1)} async-done(((bf16[32,2,64,128]{3,2,1,0:T(8,128)(2,1)}), bf16[32,2,64,128]{3,2,1,0:T(8,128)(2,1)S(1)}, u32[]{:S(2)}, u32[]{:S(2)}) %all-to-all-start.3) | async-done | bytes 1048608 | tf_op jit(solution)/shard_map/all_to_all | solution.py:68
  114.3 5.7 %finish.1 = (bf16[1024,128]{1,0:T(8,128)(2,1)S(1)}, f32[128,2048]{1,0:T(8,128)}) custom-call(bf16[32,2,64,128]{3,2,1,0:T(8,128)(2,1)S(1)} %all-to-all-done.3.recv, f32[4,128,2048]{2,1,0:T(8,128)} %copy-done, bf16[128,2048]{1,0:T(8,128)(2,1)S(1)} %get-tuple-element.35.nt_in.nt, bf16[128,2048]{1,0:T(8,128)(2,1)} %get-tuple-element.40.gg.gg_h, ...), custom_call_target="tpu_custom_call" | custom-call | flops 500000000 | bytes 10485760 | tf_op jit(solution)/shard_map/finish/pallas_call | solution.py:42
  120.0 14.6 %all_to_all.32.recv = bf16[32,32,128]{2,1,0:T(8,128)(2,1)S(1)} all-to-all(bf16[32,32,128]{2,1,0:T(8,128)(2,1)S(1)} %bitcast.7), channel_id=1, replica_groups=mesh['row'=8,'col'=4] {'row','col'}, dimensions={0} | all-to-all | bytes 524288 | tf_op jit(solution)/shard_map/all_to_all | solution.py:68
  134.6 0.7 add_up.1
  135.3 2.7 %all-to-all-start.5 = ((bf16[32,32,128]{2,1,0:T(8,128)(2,1)}), bf16[32,32,128]{2,1,0:T(8,128)(2,1)S(1)}, u32[]{:S(2)}, u32[]{:S(2)}) async-start(bf16[32,32,128]{2,1,0:T(8,128)(2,1)} %add_up.1), calls=%async_computation.5 | async-start | bytes 524288 | tf_op jit(solution)/shard_map/all_to_all | solution.py:68
  138.0 0.0 copy-done.2
  138.0 0.0 copy-done.18
  138.0 0.0 copy-start.4
  138.0 1.2 copy-done.4
  139.2 2.1 %close.1 = bf16[32,64,128]{2,1,0:T(8,128)(2,1)} custom-call(f32[128,2048]{1,0:T(8,128)S(1)} %copy-done.4, f32[128,2048]{1,0:T(8,128)S(1)} %copy-done.2, f32[8,2048]{1,0:T(8,128)S(1)} %get-tuple-element.52.scale, f32[1,128]{1,0:T(1,128)S(1)} %bitcast.9), custom_call_target="tpu_custom_call" | custom-call | flops 50000000 | bytes 3145728 | tf_op jit(solution)/shard_map/close/pallas_call | solution.py:42
  141.4 6.8 %all-to-all-done.5 = bf16[32,32,128]{2,1,0:T(8,128)(2,1)S(1)} async-done(((bf16[32,32,128]{2,1,0:T(8,128)(2,1)}), bf16[32,32,128]{2,1,0:T(8,128)(2,1)S(1)}, u32[]{:S(2)}, u32[]{:S(2)}) %all-to-all-start.5) | async-done | bytes 262176 | tf_op jit(solution)/shard_map/all_to_all | solution.py:68
  148.2 0.8 deliver.1
  (13 shorter events, 0.0 us)
Async XLA Ops:
  0.6 44.7 %copy-start.13 = (bf16[128,256]{1,0:T(8,128)(2,1)S(1)}, bf16[128,256]{1,0:T(8,128)(2,1)}, u32[]{:S(2)}) copy-start(bf16[128,256]{1,0:T(8,128)(2,1)} %rw.3) | copy-start | bytes 196612
  0.6 44.7 %copy-start.12 = (bf16[128,256]{1,0:T(8,128)(2,1)S(1)}, bf16[128,256]{1,0:T(8,128)(2,1)}, u32[]{:S(2)}) copy-start(bf16[128,256]{1,0:T(8,128)(2,1)} %lw.3) | copy-start | bytes 196612
  0.7 44.7 %copy-start.6 = (bf16[32,64,128]{2,1,0:T(8,128)(2,1)S(1)}, bf16[32,64,128]{2,1,0:T(8,128)(2,1)}, u32[]{:S(2)}) copy-start(bf16[32,64,128]{2,1,0:T(8,128)(2,1)} %pair.1) | copy-start | bytes 1572868
  0.7 44.7 %copy-start.14 = (bf16[128,128]{1,0:T(8,128)(2,1)S(1)}, bf16[128,128]{1,0:T(8,128)(2,1)}, u32[]{:S(2)}) copy-start(bf16[128,128]{1,0:T(8,128)(2,1)} %gw.3) | copy-start | bytes 98308
  0.7 44.7 %copy-start.7 = (bf16[32,64,128]{2,1,0:T(8,128)(2,1)S(1)}, bf16[32,64,128]{2,1,0:T(8,128)(2,1)}, u32[]{:S(2)}) copy-start(bf16[32,64,128]{2,1,0:T(8,128)(2,1)} %cot.1) | copy-start | bytes 1572868
  0.7 58.9 %copy-start.17 = (bf16[128,128]{1,0:T(8,128)(2,1)S(1)}, bf16[128,128]{1,0:T(8,128)(2,1)}, u32[]{:S(2)}) copy-start(bf16[128,128]{1,0:T(8,128)(2,1)} %ow.1) | copy-start | bytes 98308
  0.7 58.9 %copy-start.20 = (f32[128]{0:T(128)S(1)}, f32[128]{0:T(128)}, u32[]{:S(2)}) copy-start(f32[128]{0:T(128)} %param.20) | copy-start | bytes 1540
  0.7 58.9 %copy-start.19 = (f32[128]{0:T(128)S(1)}, f32[128]{0:T(128)}, u32[]{:S(2)}) copy-start(f32[128]{0:T(128)} %param.19) | copy-start | bytes 1540
  40.8 18.8 %all-to-all-start.1 = ((bf16[32,64,128]{2,1,0:T(8,128)(2,1)}), bf16[32,64,128]{2,1,0:T(8,128)(2,1)S(1)}, u32[]{:S(2)}, u32[]{:S(2)}) async-start(bf16[32,64,128]{2,1,0:T(8,128)(2,1)} %get-tuple-element.34), calls=%async_computation.1 | async-start | bytes 1048576 | tf_op jit(solution)/shard_map/all_to_all | solution.py:68
  48.0 2.0 %copy-start = (f32[4,128,2048]{2,1,0:T(8,128)}, f32[4,128,2048]{2,1,0:T(8,128)S(1)}, u32[]{:S(2)}) copy-start(f32[4,128,2048]{2,1,0:T(8,128)S(1)} %get-tuple-element.47.coef_h) | copy-start | bytes 12582916
  49.9 1.0 copy-start.1
  51.0 1.0 copy-start.5
  52.0 0.8 copy-start.11
  64.5 24.9 %copy-start.15 = (f32[2,128,128]{2,1,0:T(8,128)}, f32[2,128,128]{2,1,0:T(8,128)S(1)}, u32[]{:S(2)}) copy-start(f32[2,128,128]{2,1,0:T(8,128)S(1)} %get-tuple-element.42.sums) | copy-start | bytes 393220
  64.5 24.9 %copy-start.3 = (bf16[128,2048]{1,0:T(8,128)(2,1)S(1)}, bf16[128,2048]{1,0:T(8,128)(2,1)}, u32[]{:S(2)}) copy-start(bf16[128,2048]{1,0:T(8,128)(2,1)} %get-tuple-element.40.gg.gg_h) | copy-start | bytes 1572868
  64.5 24.9 %copy-start.8 = (bf16[128,2048]{1,0:T(8,128)(2,1)S(1)}, bf16[128,2048]{1,0:T(8,128)(2,1)}, u32[]{:S(2)}) copy-start(bf16[128,2048]{1,0:T(8,128)(2,1)} %get-tuple-element.38.upd) | copy-start | bytes 1572868
  85.2 29.1 %all-to-all-start.3 = ((bf16[32,2,64,128]{3,2,1,0:T(8,128)(2,1)}), bf16[32,2,64,128]{3,2,1,0:T(8,128)(2,1)S(1)}, u32[]{:S(2)}, u32[]{:S(2)}) async-start(bf16[32,2,64,128]{3,2,1,0:T(8,128)(2,1)} %multiply_back.1), calls=%async_computation.3 | async-start | bytes 2097152 | tf_op jit(solution)/shard_map/all_to_all | solution.py:68
  89.4 1.0 copy-start.9
  90.4 1.0 copy-start.10
  91.5 0.9 copy-start.16
  114.3 23.7 %copy-start.2 = (f32[128,2048]{1,0:T(8,128)S(1)}, f32[128,2048]{1,0:T(8,128)}, u32[]{:S(2)}) copy-start(f32[128,2048]{1,0:T(8,128)} %copy-done.1) | copy-start | bytes 3145732
  114.3 23.7 %copy-start.18 = (f32[128]{0:T(128)S(1)}, f32[128]{0:T(128)}, u32[]{:S(2)}) copy-start(f32[128]{0:T(128)} %param.14) | copy-start | bytes 1540
  135.3 12.9 %all-to-all-start.5 = ((bf16[32,32,128]{2,1,0:T(8,128)(2,1)}), bf16[32,32,128]{2,1,0:T(8,128)(2,1)S(1)}, u32[]{:S(2)}, u32[]{:S(2)}) async-start(bf16[32,32,128]{2,1,0:T(8,128)(2,1)} %add_up.1), calls=%async_computation.5 | async-start | bytes 524288 | tf_op jit(solution)/shard_map/all_to_all | solution.py:68
  138.0 1.2 copy-start.4

commit v3 on v2

--- a/solution.py
+++ b/solution.py
@@ -136,7 +136,7 @@
 
     for g in range(GROUPS):
         finish_all(tiles[2 * g : 2 * g + 2])
-        lax.fori_loop(g * step_rows, (g + 1) * step_rows, step, 0, unroll=2)
+        lax.fori_loop(g * step_rows, (g + 1) * step_rows, step, 0, unroll=4)
 
     def pack(d, carry):
         at = pl.ds(pl.multiple_of(d * per, per), per)
@@ -201,17 +201,17 @@
                 out[h, row : row + half, lane : lane + LANES] = block
 
             gather_whole(n_row, n_col, half, lambda d, side=side: recv[d, side, at, :], write)
-        acc[...] = dot(left[h], right[h], NT)
+        acc[h] = dot(left[h], right[h], NT)
 
         def put(d, block):
             send[d, at, :] = block.astype(BF16)
 
-        scatter_tiles(n_row, n_col, half, acc, put)
+        scatter_tiles(n_row, n_col, half, acc.at[h], put)
         begin(send.at[:, at], send_h.at[:, at], sems.at[h])
         return carry
 
     own = left.shape[0]
-    lax.fori_loop(0, own, step, 0)
+    lax.fori_loop(0, own, step, 0, unroll=True)
     for h in range(own):
         at = span(h, half)
         pltpu.make_async_copy(send.at[:, at], send_h.at[:, at], sems.at[h]).wait()
@@ -222,22 +222,22 @@
         at = pl.ds(pl.multiple_of(h * half, half), half)
 
         def write(row, lane, block):
-            grad[row : row + half, lane : lane + LANES] = block
+            grad[h, row : row + half, lane : lane + LANES] = block
 
         gather_whole(n_row, n_col, half, lambda d: recv[d, at, :], write)
-        acc[0] = dot(grad[...], right[h], NN)
-        acc[1] = dot(grad[...], left[h], TN)
+        acc[h, 0] = dot(grad[h], right[h], NN)
+        acc[h, 1] = dot(grad[h], left[h], TN)
         for side in (0, 1):
 
             def put(d, block, side=side):
                 send[d, side, at, :] = block.astype(BF16)
 
-            scatter_tiles(n_row, n_col, half, acc.at[side], put)
+            scatter_tiles(n_row, n_col, half, acc.at[h, side], put)
         begin(send.at[:, :, at], send_h.at[:, :, at], sems.at[h])
         return carry
 
     own = left.shape[0]
-    lax.fori_loop(0, own, step, 0)
+    lax.fori_loop(0, own, step, 0, unroll=True)
     for h in range(own):
         at = span(h, half)
         pltpu.make_async_copy(send.at[:, :, at], send_h.at[:, :, at], sems.at[h]).wait()
@@ -255,7 +255,7 @@
     lax.fori_loop(0, n_dev, step, 0, unroll=4)
 
 
-def middle(half, hidden, recv, gate_h, cot_h, gain, bias, ow, send, upd_h, og_h, gg_h, tn_h, sums, gate_in, cot_in, upd, og_out, gg_out, tn_out, scr, owt, gb, sems, out_sems):
+def middle(half, hidden, recv, gate_h, cot_h, gain, bias, ow, send, outer_h, og_h, tn_h, sums, gate_in, cot_in, outer_out, og_out, tn_out, scr, owt, gb, sems, out_sems):
     n_dev, per, _ = send.shape
     size = gate_in.shape[1] // GROUPS
     fetched = []
@@ -278,10 +278,9 @@
         outer = dot(owt[...], tn)
         gate = gate_in[:, at]
         up = cot_in[:, at].astype(F32)
-        upd[:, at] = (gate * outer).astype(BF16)
+        outer_out[:, at] = outer
         og = (up * gate).astype(BF16)
         og_out[:, at] = og
-        gg_out[:, at] = (up * outer * gate * (1.0 - gate)).astype(BF16)
         tg = dot(ow[...], og)
         sums[0] += tg * hat
         sums[1] += tg
@@ -292,14 +291,14 @@
         return carry
 
     stored = []
-    saved = ((upd, upd_h), (og_out, og_h), (gg_out, gg_h), (tn_out, tn_h))
+    saved = ((outer_out, outer_h), (og_out, og_h), (tn_out, tn_h))
     for g in range(GROUPS):
         finish_all(fetched[2 * g : 2 * g + 2])
         count = half // GROUPS
-        lax.fori_loop(g * count, (g + 1) * count, step, 0, unroll=2)
+        lax.fori_loop(g * count, (g + 1) * count, step, 0, unroll=4)
         at = span(g, size)
         for k, (source, target) in enumerate(saved):
-            stored.append(begin(source.at[:, at], target.at[:, at], out_sems.at[4 * g + k]))
+            stored.append(begin(source.at[:, at], target.at[:, at], out_sems.at[3 * g + k]))
 
     def pack(d, carry):
         at = pl.ds(pl.multiple_of(d * per, per), per)
@@ -314,110 +313,86 @@
     return jnp.sum(x.T, axis=0, keepdims=True)
 
 
-def settle(half, upd, og, gg, tn, nt, sums, update, early, norms):
+def settle(half, outer_h, gate_h, cot_h, og_h, tn_h, nt, sums, update, gg_h, early, norms, outer, gate, cot, og, tn, gg, sems):
+    pairs = ((outer_h, outer), (gate_h, gate), (cot_h, cot), (og_h, og), (tn_h, tn))
+    finish_all([begin(a, b, sems.at[k]) for k, (a, b) in enumerate(pairs)])
+
     def step(p, carry):
         at = pl.ds(pl.multiple_of(p * LANES, LANES), LANES)
-        tile = upd[:, at].astype(F32).T.astype(BF16)
+        g, o = gate[:, at], outer[:, at]
+        tile = (g * o).T.astype(BF16)
         cols = update.shape[1]
         update[p] = tile[:cols]
         update[half + p] = tile[cols:]
+        gg[:, at] = (cot[:, at].astype(F32) * o * g * (1.0 - g)).astype(BF16)
         return carry
 
     lax.fori_loop(0, half, step, 0, unroll=2)
+    stored = begin(gg, gg_h, sems.at[len(pairs)])
     early[0] = dot(nt[...], gg[...], NT)
     early[1] = dot(tn[...], og[...], NT)
     norms[0:1] = fold(sums[0])
     norms[1:2] = fold(sums[1])
-
-
-def finish(half, hidden, recv, coef_h, nt, gg_h, hat_h, lw, rw, gw, early, early_norms, parts, ng_h, coef, gg, hat, ng_out, scr, comb, sums, sems, out_sems):
-    size = hat.shape[1] // GROUPS
+    stored.wait()
+
+
+def finish(half, hidden, recv, coef_h, nt, early, parts, comb_h, coef, comb, scr, sems, out_sems):
+    size = nt.shape[1] // GROUPS
     fetched = []
     for g in range(GROUPS):
         at = span(g, size)
-        fetched.append(begin(coef_h.at[:, :, at], coef.at[:, :, at], sems.at[3 * g]))
-        fetched.append(begin(gg_h.at[:, at], gg.at[:, at], sems.at[3 * g + 1]))
-        fetched.append(begin(hat_h.at[:, at], hat.at[:, at], sems.at[3 * g + 2]))
+        fetched.append(begin(coef_h.at[:, :, at], coef.at[:, :, at], sems.at[g]))
     for side in (0, 1):
         unpack(recv, scr.at[side], side)
-    sums[...] = jnp.zeros_like(sums)
 
     def step(p, carry):
         at = pl.ds(pl.multiple_of(p * LANES, LANES), LANES)
         rows = pl.ds(p, hidden, stride=half)
-        ng = dot(gw[...], gg[:, at])
-        for side, w in ((0, lw), (1, rw)):
+        for side in (0, 1):
             part = scr[side, rows, :]
-            both = jnp.concatenate(
-                [part * coef[2 * side, :, at], part * coef[2 * side + 1, :, at]], axis=0
-            ).astype(BF16)
-            comb[side, :, at] = both
-            ng = ng + dot(w[...], both)
-        ng_out[:, at] = ng
-        sums[0] += ng * hat[:, at]
-        sums[1] += ng
+            comb[side, :hidden, at] = (part * coef[2 * side, :, at]).astype(BF16)
+            comb[side, hidden:, at] = (part * coef[2 * side + 1, :, at]).astype(BF16)
         return carry
 
     stored = []
     for g in range(GROUPS):
-        finish_all(fetched[3 * g : 3 * g + 3])
+        fetched[g].wait()
         count = half // GROUPS
-        lax.fori_loop(g * count, (g + 1) * count, step, 0, unroll=2)
+        lax.fori_loop(g * count, (g + 1) * count, step, 0, unroll=4)
         at = span(g, size)
-        stored.append(begin(ng_out.at[:, at], ng_h.at[:, at], out_sems.at[g]))
+        stored.append(begin(comb.at[:, :, at], comb_h.at[:, :, at], out_sems.at[g]))
     c = nt.shape[0]
-    parts[...] = jnp.zeros_like(parts)
+    base = 5 * c + hidden
     for side in (0, 1):
         grad = dot(nt[...], comb[side], NT)
         parts[2 * side * c : (2 * side + 1) * c] = grad[:, :hidden].astype(BF16)
         parts[(2 * side + 1) * c : (2 * side + 2) * c] = grad[:, hidden:].astype(BF16)
     parts[4 * c : 5 * c] = early[0].astype(BF16)
-    parts[5 * c : 5 * c + hidden] = early[1].astype(BF16)
-    exact = jnp.concatenate([fold(sums[0]), fold(sums[1]), early_norms[0:2]], axis=0)
-    high = exact.astype(BF16)
-    low = (exact - high.astype(F32)).astype(BF16)
-    base = 5 * c + hidden
-    parts[base : base + 8] = jnp.concatenate([high, low], axis=0)
+    parts[5 * c : base] = early[1].astype(BF16)
+    if parts.shape[0] > base:
+        parts[base:] = jnp.zeros((parts.shape[0] - base, LANES), BF16)
     finish_all(stored)
 
 
-def add_up(scale, holder, n_col, recv, send):
-    n_dev, share, _ = recv.shape
-    mine = scale * jnp.sum(recv[...].astype(F32), axis=0)
-    exact = mine[0:4] + mine[4:8]
-    high = exact.astype(BF16).astype(F32)
-    pairs = jnp.concatenate([high, exact - high], axis=0)
-    if share > 8:
-        pairs = jnp.concatenate([pairs, mine[8:]], axis=0)
-    keep = (lax.axis_index("row") * n_col + lax.axis_index("col") == holder).astype(F32)
-    result = (keep * pairs + (1.0 - keep) * mine).astype(BF16)
-    for d in range(n_dev):
-        send[d] = result
-
-
-def deliver(totals, left, right, gating, output, norms):
-    c = left.shape[0]
-
-    def rows(k, n=c):
-        return totals[k * c : k * c + n].astype(F32)
-
-    for k, out in ((0, left), (2, right)):
-        out[:, :LANES] = rows(k)
-        out[:, LANES:] = rows(k + 1)
-    gating[...] = rows(4)
-    output[...] = rows(5)
-    exact = rows(6, 8)
-    norms[...] = exact[0:4] + exact[4:8]
-
-
-def close(half, ng, hat, scale, gain, grad_pair, gb):
+def close(half, comb_h, gg_h, hat_h, scale, gain, lw, rw, gw, early_norms, grad_pair, pairs, comb, gg, hat, sums, gb, sems):
+    size = gg.shape[1] // GROUPS
+    fetched = []
+    for g in range(GROUPS):
+        at = span(g, size)
+        fetched.append(begin(comb_h.at[:, :, at], comb.at[:, :, at], sems.at[3 * g]))
+        fetched.append(begin(gg_h.at[:, at], gg.at[:, at], sems.at[3 * g + 1]))
+        fetched.append(begin(hat_h.at[:, at], hat.at[:, at], sems.at[3 * g + 2]))
     gb[...] = column(gain[...])
+    sums[...] = jnp.zeros_like(sums)
     cols = grad_pair.shape[1]
 
     def step(p, carry):
         at = pl.ds(pl.multiple_of(p * LANES, LANES), LANES)
-        q = ng[:, at] * gb[...]
         h = hat[:, at]
+        ng = dot(gw[...], gg[:, at]) + dot(lw[...], comb[0, :, at]) + dot(rw[...], comb[1, :, at])
+        sums[0] += ng * h
+        sums[1] += ng
+        q = ng * gb[...]
         back = q - jnp.mean(q, axis=0, keepdims=True)
         back = back - h * jnp.mean(q * h, axis=0, keepdims=True)
         tile = (scale[0:1, at] * back).T.astype(BF16)
@@ -425,7 +400,37 @@
         grad_pair[half + p] = tile[cols:]
         return carry
 
-    lax.fori_loop(0, half, step, 0, unroll=2)
+    for g in range(GROUPS):
+        finish_all(fetched[3 * g : 3 * g + 3])
+        count = half // GROUPS
+        lax.fori_loop(g * count, (g + 1) * count, step, 0, unroll=2)
+    exact = jnp.concatenate([fold(sums[0]), fold(sums[1]), early_norms[0:2]], axis=0)
+    high = exact.astype(BF16)
+    pairs[...] = jnp.concatenate([high, (exact - high.astype(F32)).astype(BF16)], axis=0)
+
+
+def add_up(scale, recv, pairs, send):
+    n_dev, share, _ = recv.shape
+    mine = (scale * jnp.sum(recv[...].astype(F32), axis=0)).astype(BF16)
+    own = pairs[...]
+    for d in range(n_dev):
+        send[d, :share] = mine
+        send[d, share:] = own
+
+
+def deliver(scale, recv, left, right, gating, output, norms, flat):
+    c = left.shape[0]
+    n_dev, share = recv.shape[0], recv.shape[1] - 8
+    total = jnp.zeros((8, LANES), F32)
+    for d in range(n_dev):
+        flat[d * share : (d + 1) * share] = recv[d, :share].astype(F32)
+        total = total + recv[d, share:].astype(F32)
+    for k, out in ((0, left), (2, right)):
+        out[:, :LANES] = flat[k * c : (k + 1) * c]
+        out[:, LANES:] = flat[(k + 1) * c : (k + 2) * c]
+    gating[...] = flat[4 * c : 5 * c]
+    output[...] = flat[5 * c : 5 * c + output.shape[0]]
+    norms[...] = scale * (total[0:4] + total[4:8])
 
 
 def per_device(
@@ -480,72 +485,71 @@
         functools.partial(multiply, n_row, n_col, half),
         (VMEM,),
         [((n_dev, per, LANES), BF16, HBM)] + [((own, tokens, tokens), BF16, VMEM)] * 2,
-        [vm((tokens, tokens), F32), vm((n_dev, per, LANES), BF16), dma((own,))],
+        [vm((own, tokens, tokens), F32), vm((n_dev, per, LANES), BF16), dma((own,))],
         "multiply", 200 * 10**6, 3 * 2**20,
     )(both)
     tri = exchange(send)
-    send, upd, og, gg, tn, sums = call(
+    send, outer, og, tn, sums = call(
         functools.partial(middle, half, hidden),
         (VMEM, HBM, HBM, VMEM, VMEM, VMEM),
-        [((n_dev, per, LANES), BF16, VMEM)] + [((c, wide), BF16, HBM)] * 4 + [((2,) + sq, F32, VMEM)],
-        [vm((c, wide), F32)] + [vm((c, wide), BF16)] * 5 + [vm((rows, LANES), F32)]
-        + [vm((c, hidden), BF16), vm((2,) + sq, F32), dma((2 * GROUPS,)), dma((4 * GROUPS,))],
+        [((n_dev, per, LANES), BF16, VMEM), ((c, wide), F32, HBM)]
+        + [((c, wide), BF16, HBM)] * 2 + [((2,) + sq, F32, VMEM)],
+        [vm((c, wide), F32), vm((c, wide), BF16), vm((c, wide), F32)]
+        + [vm((c, wide), BF16)] * 2 + [vm((rows, LANES), F32)]
+        + [vm((c, hidden), BF16), vm((2,) + sq, F32), dma((2 * GROUPS,)), dma((3 * GROUPS,))],
         "middle", 200 * 10**6, 6 * 2**20,
     )(tri, gate, cot, o_gain, o_bias, out_weight)
     grad = exchange(send)
-    update, early, early_norms = call(
+    update, gg, early, early_norms = call(
         functools.partial(settle, half),
-        (VMEM,) * 6,
-        [((rows_dev, cols_dev, c), BF16, VMEM), ((2,) + sq, F32, VMEM), ((8, LANES), F32, VMEM)],
-        [],
+        (HBM,) * 5 + (VMEM,) * 2,
+        [((rows_dev, cols_dev, c), BF16, VMEM), ((c, wide), BF16, HBM)]
+        + [((2,) + sq, F32, VMEM), ((8, LANES), F32, VMEM)],
+        [vm((c, wide), F32)] * 2 + [vm((c, wide), BF16)] * 4 + [dma((6,))],
         "settle", 200 * 10**6, 4 * 2**20,
-    )(upd, og, gg, tn, nt, sums)
+    )(outer, gate, cot, og, tn, nt, sums)
     (send,) = call(
         functools.partial(multiply_back, n_row, n_col, half),
         (VMEM,) * 3,
         [((n_dev, 2, per, LANES), BF16, HBM)],
-        [vm((tokens, tokens), BF16), vm((2, tokens, tokens), F32)]
+        [vm((own, tokens, tokens), BF16), vm((own, 2, tokens, tokens), F32)]
         + [vm((n_dev, 2, per, LANES), BF16), dma((own,))],
         "multiply_back", 300 * 10**6, 3 * 2**20,
     )(grad, left, right)
     back = exchange(send)
-    base = 5 * c + hidden
-    assert base % 8 == 0
-    share = -(-(base + 8) // (n_dev * 8)) * 8
-    while base % share:
-        share += 8
-    parts, ng = call(
+    share = -(-(5 * c + hidden) // (n_dev * 8)) * 8
+    parts, comb = call(
         functools.partial(finish, half, hidden),
-        (VMEM, HBM, VMEM, HBM, HBM) + (VMEM,) * 5,
-        [((n_dev * share, LANES), BF16, VMEM), ((c, wide), F32, HBM)],
-        [vm((4, hidden, wide), F32), vm((c, wide), BF16), vm((c, wide), F32), vm((c, wide), F32)]
-        + [vm((2, rows, LANES), F32), vm((2, 2 * hidden, wide), BF16), vm((2,) + sq, F32)]
-        + [dma((3 * GROUPS,)), dma((GROUPS,))],
-        "finish", 500 * 10**6, 10 * 2**20,
-    )(back, coef, nt, gg, hat, left_weight, right_weight, gate_weight, early, early_norms)
+        (VMEM, HBM, VMEM, VMEM),
+        [((n_dev * share, LANES), BF16, VMEM), ((2, 2 * hidden, wide), BF16, HBM)],
+        [vm((4, hidden, wide), F32), vm((2, 2 * hidden, wide), BF16), vm((2, rows, LANES), F32)]
+        + [dma((GROUPS,)), dma((GROUPS,))],
+        "finish", 300 * 10**6, 8 * 2**20,
+    )(back, coef, nt, early)
+    summed = exchange(parts.reshape(n_dev, share, LANES))
+    grad_pair, pairs = call(
+        functools.partial(close, half),
+        (HBM,) * 3 + (VMEM,) * 6,
+        [((rows_dev, cols_dev, c), BF16, VMEM), ((8, LANES), BF16, VMEM)],
+        [vm((2, 2 * hidden, wide), BF16), vm((c, wide), BF16), vm((c, wide), F32)]
+        + [vm((2,) + sq, F32), vm(sq, F32), dma((3 * GROUPS,))],
+        "close", 300 * 10**6, 6 * 2**20,
+    )(comb, gg, hat, scale, gain, left_weight, right_weight, gate_weight, early_norms)
     (send,) = call(
-        functools.partial(add_up, 1.0 / tokens, base // share, n_col),
-        (VMEM,),
-        [((n_dev, share, LANES), BF16, VMEM)],
+        functools.partial(add_up, 1.0 / tokens),
+        (VMEM, VMEM),
+        [((n_dev, share + 8, LANES), BF16, VMEM)],
         [],
         "add_up", 10**6, 2**19,
-    )(exchange(parts.reshape(n_dev, share, LANES)))
-    totals = exchange(send).reshape(n_dev * share, LANES)
-    (grad_pair,) = call(
-        functools.partial(close, half),
-        (VMEM,) * 4,
-        [((rows_dev, cols_dev, c), BF16, VMEM)],
-        [vm(sq, F32)],
-        "close", 50 * 10**6, 3 * 2**20,
-    )(ng, hat, scale, gain)
+    )(summed, pairs)
     grads = call(
-        deliver,
+        functools.partial(deliver, 1.0 / tokens),
         (VMEM,),
         [((c, 2 * hidden), F32, VMEM)] * 2
         + [((c, c), F32, VMEM), ((hidden, c), F32, VMEM), ((4, c), F32, VMEM)],
-        [],
+        [vm((n_dev * share, LANES), F32)],
         "deliver", 10**6, 2**20,
-    )(totals)
+    )(exchange(send))
     return (update, grad_pair) + tuple(grads)
 
 

time: 150 us -> 143 us (0.953)
  local copies, waits for them, and re-layouts: 9.02 us -> 4.73 us
  waiting for transfers between devices: 34 us -> 31.1 us
  blocking collectives: 64.9 us -> 62.5 us
  starting transfers between devices: 11.4 us -> 13.3 us
    unnamed x42 -> x26, local copies, waits for them, and re-layouts: 9.02 us -> 4.73 us
    all_to_all x3, waiting for transfers between devices: 34 us -> 31.1 us  [exchange(): return lax.all_to_all(blocks, BOTH, split_axis=0, concat_axis=0, tiled=True)]
    all_to_all x3, blocking collectives: 64.9 us -> 62.5 us  [exchange(): return lax.all_to_all(blocks, BOTH, split_axis=0, concat_axis=0, tiled=True)]
    all_to_all x3, starting transfers between devices: 11.4 us -> 13.3 us  [exchange(): return lax.all_to_all(blocks, BOTH, split_axis=0, concat_axis=0, tiled=True)]
  transfers between devices with their start and end apart: 3 -> 3, of which waited for: 3 -> 3; matrix products, arithmetic and copies ran while one was open for 0% -> 0% of each run, Pallas kernels for 4% -> 9%
where the time goes in v3:
time: 143 us; the launch traced here: 142 us
  blocking collectives  62.5 us (44%)
  waiting for transfers between devices  31.1 us (22%)
  Pallas kernels  29.2 us (20%)
  starting transfers between devices  13.3 us (9%)
  local copies, waits for them, and re-layouts  4.73 us (3%)
  between operations  1.6 us (1%)
    all_to_all x3, blocking collectives, exchange(): return lax.all_to_all(blocks, BOTH, split_axis=0, concat_axis=0, tiled=True)  62.5 us
    all_to_all x3, waiting for transfers between devices, exchange(): return lax.all_to_all(blocks, BOTH, split_axis=0, concat_axis=0, tiled=True)  31.1 us
    pallas_call x10, Pallas kernels, placed(): run(*[pltpu.with_memory_space_constraint(x, pltpu.HBM) if spec is HBM els...  29.2 us
    all_to_all x3, starting transfers between devices, exchange(): return lax.all_to_all(blocks, BOTH, split_axis=0, concat_axis=0, tiled=True)  13.3 us
    unnamed x26, local copies, waits for them, and re-layouts  4.73 us
  transfers between devices with their start and end apart: 3, of which 3 were waited for; matrix products, arithmetic and copies ran while one was open for 0% of the time, Pallas kernels for 9%

profile of v3, /device:TPU:0, one launch (start us, length us, event | category | flops | bytes accessed | tf_op | source)
XLA Modules:
  0.0 142.5 jit_solution(17398919366228153435)
XLA Ops:
  0.6 0.0 copy-start.7
  0.6 0.0 copy-start.6
  0.7 0.0 copy-start.4
  0.7 0.0 copy-start.8
  0.7 0.0 copy-start.5
  0.7 0.0 copy-start.9
  0.7 0.0 copy-start.12
  0.7 0.0 copy-start.11
  1.4 3.9 %project.1 = (bf16[32,2,64,128]{3,2,1,0:T(8,128)(2,1)S(1)}, bf16[128,2048]{1,0:T(8,128)(2,1)S(1)}) custom-call(s32[1]{0:T(128)S(6)} %copy.18.length, bf16[32,64,128]{2,1,0:T(8,128)(2,1)} %pair.1, f32[1,128]{1,0:T(1,128)} %bitcast.5, f32[1,128]{1,0:T(1,128)} %bitcast.9, bf16[128,256]{1,0:T(8,128)(2,1)} %lw.3, bf16[128,256]{1,0:T(8,128)(2,1)} %rw.3), custom_call_target="tpu_custom_call" | custom-call | flops 300000000 | bytes 3145728 | tf_op jit(solution)/shard_map/project/pallas_call | solution.py:42
  5.3 32.1 %all_to_all.30.recv = bf16[32,2,64,128]{3,2,1,0:T(8,128)(2,1)S(1)} all-to-all(bf16[32,2,64,128]{3,2,1,0:T(8,128)(2,1)S(1)} %get-tuple-element.35), channel_id=1, replica_groups=mesh['row'=8,'col'=4] {'row','col'}, dimensions={0} | all-to-all | bytes 2097152 | tf_op jit(solution)/shard_map/all_to_all | solution.py:68
  37.4 1.5 %multiply.1 = (bf16[32,64,128]{2,1,0:T(8,128)(2,1)}, bf16[4,256,256]{2,1,0:T(8,128)(2,1)S(1)}, bf16[4,256,256]{2,1,0:T(8,128)(2,1)S(1)}) custom-call(bf16[32,2,64,128]{3,2,1,0:T(8,128)(2,1)S(1)} %all_to_all.30.recv), custom_call_target="tpu_custom_call" | custom-call | flops 200000000 | bytes 3145728 | tf_op jit(solution)/shard_map/multiply/pallas_call | solution.py:42
  38.9 4.6 %all-to-all-start.1 = ((bf16[32,64,128]{2,1,0:T(8,128)(2,1)}), bf16[32,64,128]{2,1,0:T(8,128)(2,1)S(1)}, u32[]{:S(2)}, u32[]{:S(2)}) async-start(bf16[32,64,128]{2,1,0:T(8,128)(2,1)} %get-tuple-element.36), calls=%async_computation.1 | async-start | bytes 1048576 | tf_op jit(solution)/shard_map/all_to_all | solution.py:68
  43.4 0.0 copy-done.7
  43.5 0.0 copy-done.6
  43.5 0.0 copy-done.4
  43.5 0.0 copy-done.8
  43.5 0.0 copy-done.5
  43.5 2.6 %prepare.1 = (f32[128,2048]{1,0:T(8,128)S(1)}, bf16[128,2048]{1,0:T(8,128)(2,1)S(1)}, f32[4,128,2048]{2,1,0:T(8,128)S(1)}, f32[128,2048]{1,0:T(8,128)S(1)}, f32[8,2048]{1,0:T(8,128)S(1)}) custom-call(s32[1]{0:T(128)S(6)} %copy.18.length, bf16[32,64,128]{2,1,0:T(8,128)(2,1)S(1)} %copy-done.4, bf16[32,64,128]{2,1,0:T(8,128)(2,1)S(1)} %copy-done.5, ...), custom_call_target="tpu_custom_call" | custom-call | flops 400000000 | bytes 9437184 | tf_op jit(solution)/shard_map/prepare/pallas_call | solution.py:42
  46.1 0.0 copy-start
  46.1 1.9 %copy-done = f32[4,128,2048]{2,1,0:T(8,128)} copy-done((f32[4,128,2048]{2,1,0:T(8,128)}, f32[4,128,2048]{2,1,0:T(8,128)S(1)}, u32[]{:S(2)}) %copy-start) | copy-done | bytes 4194328
  48.0 0.0 copy-start.1
  48.0 1.0 copy-done.1
  49.0 0.0 copy-start.2
  49.0 0.8 copy-done.2
  49.8 0.0 copy-start.3
  49.8 1.0 copy-done.3
  50.8 6.9 %all-to-all-done.1.recv = bf16[32,64,128]{2,1,0:T(8,128)(2,1)S(1)} async-done(((bf16[32,64,128]{2,1,0:T(8,128)(2,1)}), bf16[32,64,128]{2,1,0:T(8,128)(2,1)S(1)}, u32[]{:S(2)}, u32[]{:S(2)}) %all-to-all-start.1) | async-done | bytes 524320 | tf_op jit(solution)/shard_map/all_to_all | solution.py:68
  57.7 0.0 copy-done.9
  57.7 0.0 copy-done.12
  57.7 0.0 copy-done.11
  57.7 4.0 %middle.1 = (bf16[32,64,128]{2,1,0:T(8,128)(2,1)S(1)}, f32[128,2048]{1,0:T(8,128)}, bf16[128,2048]{1,0:T(8,128)(2,1)}, bf16[128,2048]{1,0:T(8,128)(2,1)}, f32[2,128,128]{2,1,0:T(8,128)S(1)}) custom-call(bf16[32,64,128]{2,1,0:T(8,128)(2,1)S(1)} %all-to-all-done.1.recv, f32[128,2048]{1,0:T(8,128)} %copy-done.1, bf16[128,2048]{1,0:T(8,128)(2,1)} %copy-done.2, ...), custom_call_target="tpu_custom_call" | custom-call | flops 200000000 | bytes 6291456 | tf_op jit(solution)/shard_map/middle/pallas_call | solution.py:42
  61.7 18.2 %all_to_all.31.recv = bf16[32,64,128]{2,1,0:T(8,128)(2,1)S(1)} all-to-all(bf16[32,64,128]{2,1,0:T(8,128)(2,1)S(1)} %get-tuple-element.45), channel_id=1, replica_groups=mesh['row'=8,'col'=4] {'row','col'}, dimensions={0} | all-to-all | bytes 1048576 | tf_op jit(solution)/shard_map/all_to_all | solution.py:68
  79.9 1.9 %multiply_back.1 = bf16[32,2,64,128]{3,2,1,0:T(8,128)(2,1)} custom-call(bf16[32,64,128]{2,1,0:T(8,128)(2,1)S(1)} %all_to_all.31.recv, bf16[4,256,256]{2,1,0:T(8,128)(2,1)S(1)} %get-tuple-element.46.left, bf16[4,256,256]{2,1,0:T(8,128)(2,1)S(1)} %get-tuple-element.47.right), custom_call_target="tpu_custom_call" | custom-call | flops 300000000 | bytes 3145728 | tf_op jit(solution)/shard_map/multiply_back/pallas_call | solution.py:42
  81.8 4.2 %all-to-all-start.3 = ((bf16[32,2,64,128]{3,2,1,0:T(8,128)(2,1)}), bf16[32,2,64,128]{3,2,1,0:T(8,128)(2,1)S(1)}, u32[]{:S(2)}, u32[]{:S(2)}) async-start(bf16[32,2,64,128]{3,2,1,0:T(8,128)(2,1)} %multiply_back.1), calls=%async_computation.3 | async-start | bytes 2097152 | tf_op jit(solution)/shard_map/all_to_all | solution.py:68
  86.0 4.6 %settle.1 = (bf16[32,64,128]{2,1,0:T(8,128)(2,1)}, bf16[128,2048]{1,0:T(8,128)(2,1)}, f32[2,128,128]{2,1,0:T(8,128)S(1)}, f32[8,128]{1,0:T(8,128)S(1)}) custom-call(f32[128,2048]{1,0:T(8,128)} %get-tuple-element.40.outer_h, f32[128,2048]{1,0:T(8,128)} %copy-done.1, bf16[128,2048]{1,0:T(8,128)(2,1)} %copy-done.2, bf16[128,2048]{1,0:T(8,128)(2,1)} %get-tuple-element.41.og_h, ...), custom_call_target="tpu_custom_call" | custom-call | flops 200000000 | bytes 4194304 | tf_op jit(solution)/shard_map/settle/pallas_call | solution.py:42
  90.6 0.0 copy-start.10
  90.6 20.3 %all-to-all-done.3.recv = bf16[32,2,64,128]{3,2,1,0:T(8,128)(2,1)S(1)} async-done(((bf16[32,2,64,128]{3,2,1,0:T(8,128)(2,1)}), bf16[32,2,64,128]{3,2,1,0:T(8,128)(2,1)S(1)}, u32[]{:S(2)}, u32[]{:S(2)}) %all-to-all-start.3) | async-done | bytes 1048608 | tf_op jit(solution)/shard_map/all_to_all | solution.py:68
  110.9 4.6 %finish.1 = (bf16[768,128]{1,0:T(8,128)(2,1)}, bf16[2,256,2048]{2,1,0:T(8,128)(2,1)}) custom-call(bf16[32,2,64,128]{3,2,1,0:T(8,128)(2,1)S(1)} %all-to-all-done.3.recv, f32[4,128,2048]{2,1,0:T(8,128)} %copy-done, bf16[128,2048]{1,0:T(8,128)(2,1)S(1)} %get-tuple-element.37.nt_in.nt, f32[2,128,128]{2,1,0:T(8,128)S(1)} %get-tuple-element.49.early), custom_call_target="tpu_custom_call" | custom-call | flops 300000000 | bytes 8388608 | tf_op jit(solution)/shard_map/finish/pallas_call | solution.py:42
  115.6 4.6 %all-to-all-start.4 = ((bf16[32,24,128]{2,1,0:T(8,128)(2,1)}), bf16[32,24,128]{2,1,0:T(8,128)(2,1)S(1)}, u32[]{:S(2)}, u32[]{:S(2)}) async-start(bf16[32,24,128]{2,1,0:T(8,128)(2,1)} %bitcast.4), calls=%async_computation.4 | async-start | bytes 393216 | tf_op jit(solution)/shard_map/all_to_all | solution.py:68
  120.1 0.0 copy-done.10
  120.2 5.4 %close.1 = (bf16[32,64,128]{2,1,0:T(8,128)(2,1)}, bf16[8,128]{1,0:T(8,128)(2,1)S(1)}) custom-call(bf16[2,256,2048]{2,1,0:T(8,128)(2,1)} %get-tuple-element.50.comb_h, bf16[128,2048]{1,0:T(8,128)(2,1)} %get-tuple-element.51.gg_h, f32[128,2048]{1,0:T(8,128)} %copy-done.3, f32[8,2048]{1,0:T(8,128)S(1)} %get-tuple-element.53.scale, f32[1,128]{1,0:T(1,128)S(1)} %bitcast.6, ...), custom_call_target="tpu_custom_call" | custom-call | flops 300000000 | bytes 6291456 | tf_op jit(solution)/shard_map/close/pallas_call | solution.py:42
  125.5 3.9 %all-to-all-done.4.recv = bf16[32,24,128]{2,1,0:T(8,128)(2,1)S(1)} async-done(((bf16[32,24,128]{2,1,0:T(8,128)(2,1)}), bf16[32,24,128]{2,1,0:T(8,128)(2,1)S(1)}, u32[]{:S(2)}, u32[]{:S(2)}) %all-to-all-start.4) | async-done | bytes 196640 | tf_op jit(solution)/shard_map/all_to_all | solution.py:68
  129.4 0.1 add_up.1
  129.5 12.2 %all_to_all.32.recv = bf16[32,32,128]{2,1,0:T(8,128)(2,1)S(1)} all-to-all(bf16[32,32,128]{2,1,0:T(8,128)(2,1)S(1)} %add_up.1), channel_id=1, replica_groups=mesh['row'=8,'col'=4] {'row','col'}, dimensions={0} | all-to-all | bytes 524288 | tf_op jit(solution)/shard_map/all_to_all | solution.py:68
  141.7 0.8 deliver.1
Async XLA Ops:
  0.6 42.8 %copy-start.7 = (bf16[128,256]{1,0:T(8,128)(2,1)S(1)}, bf16[128,256]{1,0:T(8,128)(2,1)}, u32[]{:S(2)}) copy-start(bf16[128,256]{1,0:T(8,128)(2,1)} %rw.3) | copy-start | bytes 196612
  0.6 42.8 %copy-start.6 = (bf16[128,256]{1,0:T(8,128)(2,1)S(1)}, bf16[128,256]{1,0:T(8,128)(2,1)}, u32[]{:S(2)}) copy-start(bf16[128,256]{1,0:T(8,128)(2,1)} %lw.3) | copy-start | bytes 196612
  0.7 42.8 %copy-start.4 = (bf16[32,64,128]{2,1,0:T(8,128)(2,1)S(1)}, bf16[32,64,128]{2,1,0:T(8,128)(2,1)}, u32[]{:S(2)}) copy-start(bf16[32,64,128]{2,1,0:T(8,128)(2,1)} %pair.1) | copy-start | bytes 1572868
  0.7 42.8 %copy-start.8 = (bf16[128,128]{1,0:T(8,128)(2,1)S(1)}, bf16[128,128]{1,0:T(8,128)(2,1)}, u32[]{:S(2)}) copy-start(bf16[128,128]{1,0:T(8,128)(2,1)} %gw.3) | copy-start | bytes 98308
  0.7 42.8 %copy-start.5 = (bf16[32,64,128]{2,1,0:T(8,128)(2,1)S(1)}, bf16[32,64,128]{2,1,0:T(8,128)(2,1)}, u32[]{:S(2)}) copy-start(bf16[32,64,128]{2,1,0:T(8,128)(2,1)} %cot.1) | copy-start | bytes 1572868
  0.7 57.0 %copy-start.9 = (bf16[128,128]{1,0:T(8,128)(2,1)S(1)}, bf16[128,128]{1,0:T(8,128)(2,1)}, u32[]{:S(2)}) copy-start(bf16[128,128]{1,0:T(8,128)(2,1)} %ow.1) | copy-start | bytes 98308
  0.7 57.0 %copy-start.12 = (f32[128]{0:T(128)S(1)}, f32[128]{0:T(128)}, u32[]{:S(2)}) copy-start(f32[128]{0:T(128)} %param.20) | copy-start | bytes 1540
  0.7 57.0 %copy-start.11 = (f32[128]{0:T(128)S(1)}, f32[128]{0:T(128)}, u32[]{:S(2)}) copy-start(f32[128]{0:T(128)} %param.19) | copy-start | bytes 1540
  38.9 18.8 %all-to-all-start.1 = ((bf16[32,64,128]{2,1,0:T(8,128)(2,1)}), bf16[32,64,128]{2,1,0:T(8,128)(2,1)S(1)}, u32[]{:S(2)}, u32[]{:S(2)}) async-start(bf16[32,64,128]{2,1,0:T(8,128)(2,1)} %get-tuple-element.36), calls=%async_computation.1 | async-start | bytes 1048576 | tf_op jit(solution)/shard_map/all_to_all | solution.py:68
  46.1 1.9 %copy-start = (f32[4,128,2048]{2,1,0:T(8,128)}, f32[4,128,2048]{2,1,0:T(8,128)S(1)}, u32[]{:S(2)}) copy-start(f32[4,128,2048]{2,1,0:T(8,128)S(1)} %get-tuple-element.48.coef_h) | copy-start | bytes 12582916
  48.0 1.0 copy-start.1
  49.0 0.8 copy-start.2
  49.8 1.0 copy-start.3
  81.8 29.1 %all-to-all-start.3 = ((bf16[32,2,64,128]{3,2,1,0:T(8,128)(2,1)}), bf16[32,2,64,128]{3,2,1,0:T(8,128)(2,1)S(1)}, u32[]{:S(2)}, u32[]{:S(2)}) async-start(bf16[32,2,64,128]{3,2,1,0:T(8,128)(2,1)} %multiply_back.1), calls=%async_computation.3 | async-start | bytes 2097152 | tf_op jit(solution)/shard_map/all_to_all | solution.py:68
  90.6 29.5 %copy-start.10 = (f32[128]{0:T(128)S(1)}, f32[128]{0:T(128)}, u32[]{:S(2)}) copy-start(f32[128]{0:T(128)} %param.14) | copy-start | bytes 1540
  115.6 13.9 %all-to-all-start.4 = ((bf16[32,24,128]{2,1,0:T(8,128)(2,1)}), bf16[32,24,128]{2,1,0:T(8,128)(2,1)S(1)}, u32[]{:S(2)}, u32[]{:S(2)}) async-start(bf16[32,24,128]{2,1,0:T(8,128)(2,1)} %bitcast.4), calls=%async_computation.4 | async-start | bytes 393216 | tf_op jit(solution)/shard_map/all_to_all | solution.py:68

commit v4 on v3

--- a/solution.py
+++ b/solution.py
@@ -131,7 +131,7 @@
         for side, scr in ((0, ls), (1, rs)):
             proj = dot(wt[side], nt)
             act = mask * jax.nn.sigmoid(proj[hidden:]) * proj[:hidden]
-            scr[pl.ds(p, hidden, stride=half), :] = act
+            scr[pl.ds(p, hidden, stride=half + 1), :] = act
         return carry
 
     for g in range(GROUPS):
@@ -139,9 +139,11 @@
         lax.fori_loop(g * step_rows, (g + 1) * step_rows, step, 0, unroll=4)
 
     def pack(d, carry):
-        at = pl.ds(pl.multiple_of(d * per, per), per)
-        send[d, 0] = ls[at, :].astype(BF16)
-        send[d, 1] = rs[at, :].astype(BF16)
+        for k in range(per // half):
+            at = pl.ds((d * (per // half) + k) * (half + 1), half)
+            to = slice(k * half, (k + 1) * half)
+            send[d, 0, to] = ls[at, :].astype(BF16)
+            send[d, 1, to] = rs[at, :].astype(BF16)
         return carry
 
     lax.fori_loop(0, n_dev, pack, 0, unroll=4)
@@ -166,8 +168,9 @@
         for side in (0, 1):
             proj = dot(wt[side], nt)
             sig = jax.nn.sigmoid(proj[hidden:])
-            coef[2 * side, :, at] = mask * sig
-            coef[2 * side + 1, :, at] = mask * proj[:hidden] * sig * (1.0 - sig)
+            coef[2 * side, :, at] = (mask * sig).astype(BF16)
+            slope = mask * proj[:hidden] * sig * (1.0 - sig)
+            coef[2 * side + 1, :, at] = slope.astype(BF16)
         return carry
 
     lax.fori_loop(0, half, step, 0, unroll=2)
@@ -243,13 +246,14 @@
         pltpu.make_async_copy(send.at[:, :, at], send_h.at[:, :, at], sems.at[h]).wait()
 
 
-def unpack(recv, scr, side=None):
+def unpack(half, recv, scr, side=None):
     n_dev, per = recv.shape[0], recv.shape[-2]
 
     def step(d, carry):
-        at = pl.ds(pl.multiple_of(d * per, per), per)
-        block = recv[d] if side is None else recv[d, side]
-        scr[at, :] = block.astype(F32)
+        block = (recv[d] if side is None else recv[d, side]).astype(F32)
+        for k in range(per // half):
+            at = pl.ds((d * (per // half) + k) * (half + 1), half)
+            scr[at, :] = block[k * half : (k + 1) * half]
         return carry
 
     lax.fori_loop(0, n_dev, step, 0, unroll=4)
@@ -263,7 +267,7 @@
         at = span(g, size)
         fetched.append(begin(gate_h.at[:, at], gate_in.at[:, at], sems.at[2 * g]))
         fetched.append(begin(cot_h.at[:, at], cot_in.at[:, at], sems.at[2 * g + 1]))
-    unpack(recv, scr)
+    unpack(half, recv, scr)
     owt[...] = flip(ow[...])
     gb[0] = column(gain[...])
     gb[1] = column(bias[...])
@@ -271,7 +275,7 @@
 
     def step(p, carry):
         at = pl.ds(pl.multiple_of(p * LANES, LANES), LANES)
-        rows = pl.ds(p, hidden, stride=half)
+        rows = pl.ds(p, hidden, stride=half + 1)
         hat, scale = normal(scr[rows, :], 0)
         tn = (hat * gb[0] + gb[1]).astype(BF16)
         tn_out[:, at] = tn
@@ -301,8 +305,9 @@
             stored.append(begin(source.at[:, at], target.at[:, at], out_sems.at[3 * g + k]))
 
     def pack(d, carry):
-        at = pl.ds(pl.multiple_of(d * per, per), per)
-        send[d] = scr[at, :].astype(BF16)
+        for k in range(per // half):
+            at = pl.ds((d * (per // half) + k) * (half + 1), half)
+            send[d, k * half : (k + 1) * half] = scr[at, :].astype(BF16)
         return carry
 
     lax.fori_loop(0, n_dev, pack, 0, unroll=4)
@@ -336,22 +341,22 @@
     stored.wait()
 
 
-def finish(half, hidden, recv, coef_h, nt, early, parts, comb_h, coef, comb, scr, sems, out_sems):
+def finish(half, hidden, recv, coef_h, nt, early, parts, comb_h, coef, comb, scr, total, sems, out_sems):
     size = nt.shape[1] // GROUPS
     fetched = []
     for g in range(GROUPS):
         at = span(g, size)
         fetched.append(begin(coef_h.at[:, :, at], coef.at[:, :, at], sems.at[g]))
     for side in (0, 1):
-        unpack(recv, scr.at[side], side)
+        unpack(half, recv, scr.at[side], side)
 
     def step(p, carry):
         at = pl.ds(pl.multiple_of(p * LANES, LANES), LANES)
-        rows = pl.ds(p, hidden, stride=half)
+        rows = pl.ds(p, hidden, stride=half + 1)
         for side in (0, 1):
             part = scr[side, rows, :]
-            comb[side, :hidden, at] = (part * coef[2 * side, :, at]).astype(BF16)
-            comb[side, hidden:, at] = (part * coef[2 * side + 1, :, at]).astype(BF16)
+            comb[side, :hidden, at] = (part * coef[2 * side, :, at].astype(F32)).astype(BF16)
+            comb[side, hidden:, at] = (part * coef[2 * side + 1, :, at].astype(F32)).astype(BF16)
         return carry
 
     stored = []
@@ -361,10 +366,14 @@
         lax.fori_loop(g * count, (g + 1) * count, step, 0, unroll=4)
         at = span(g, size)
         stored.append(begin(comb.at[:, :, at], comb_h.at[:, :, at], out_sems.at[g]))
+        here = slice(g * size, (g + 1) * size)
+        for side in (0, 1):
+            part = dot(nt[:, here], comb[side, :, here], NT)
+            total[side] = part if g == 0 else total[side] + part
     c = nt.shape[0]
     base = 5 * c + hidden
     for side in (0, 1):
-        grad = dot(nt[...], comb[side], NT)
+        grad = total[side]
         parts[2 * side * c : (2 * side + 1) * c] = grad[:, :hidden].astype(BF16)
         parts[(2 * side + 1) * c : (2 * side + 2) * c] = grad[:, hidden:].astype(BF16)
     parts[4 * c : 5 * c] = early[0].astype(BF16)
@@ -461,7 +470,7 @@
     o_gain, o_bias = out_gain[None], out_bias[None]
     vm, dma = pltpu.VMEM, pltpu.SemaphoreType.DMA
     sq = (c, LANES)
-    rows = hidden * half
+    rows = hidden * (half + 1)
 
     send, nt = call(
         functools.partial(project, half, hidden),
@@ -476,7 +485,7 @@
     gate, cot, coef, hat, scale = call(
         functools.partial(prepare, half, hidden),
         (SMEM,) + (VMEM,) * 6,
-        [((c, wide), F32, VMEM), ((c, wide), BF16, VMEM), ((4, hidden, wide), F32, VMEM)]
+        [((c, wide), F32, VMEM), ((c, wide), BF16, VMEM), ((4, hidden, wide), BF16, VMEM)]
         + [((c, wide), F32, VMEM), ((8, wide), F32, VMEM)],
         [vm((2, 2 * hidden, c), BF16), vm((c, c), BF16)],
         "prepare", 400 * 10**6, 9 * 2**20,
@@ -522,8 +531,8 @@
         functools.partial(finish, half, hidden),
         (VMEM, HBM, VMEM, VMEM),
         [((n_dev * share, LANES), BF16, VMEM), ((2, 2 * hidden, wide), BF16, HBM)],
-        [vm((4, hidden, wide), F32), vm((2, 2 * hidden, wide), BF16), vm((2, rows, LANES), F32)]
-        + [dma((GROUPS,)), dma((GROUPS,))],
+        [vm((4, hidden, wide), BF16), vm((2, 2 * hidden, wide), BF16), vm((2, rows, LANES), F32)]
+        + [vm((2, c, 2 * hidden), F32), dma((GROUPS,)), dma((GROUPS,))],
         "finish", 300 * 10**6, 8 * 2**20,
     )(back, coef, nt, early)
     summed = exchange(parts.reshape(n_dev, share, LANES))

time: 143 us -> 140 us (0.979)
  Pallas kernels: 29.2 us -> 26.7 us
    pallas_call x10, Pallas kernels: 29.2 us -> 26.7 us  [placed(): run(*[pltpu.with_memory_space_constraint(x, pltpu.HBM) if spec is HBM els...]
where the time goes in v4:
time: 140 us
  blocking collectives  62.5 us (45%)
  waiting for transfers between devices  31.8 us (23%)
  Pallas kernels  26.7 us (19%)
  starting transfers between devices  13.3 us (10%)
  local copies, waits for them, and re-layouts  4.15 us (3%)
  between operations  1.48 us (1%)
    all_to_all x3, blocking collectives, exchange(): return lax.all_to_all(blocks, BOTH, split_axis=0, concat_axis=0, tiled=True)  62.5 us
    all_to_all x3, waiting for transfers between devices, exchange(): return lax.all_to_all(blocks, BOTH, split_axis=0, concat_axis=0, tiled=True)  31.8 us
    pallas_call x10, Pallas kernels, placed(): run(*[pltpu.with_memory_space_constraint(x, pltpu.HBM) if spec is HBM els...  26.7 us
    all_to_all x3, starting transfers between devices, exchange(): return lax.all_to_all(blocks, BOTH, split_axis=0, concat_axis=0, tiled=True)  13.3 us
    unnamed x26, local copies, waits for them, and re-layouts  4.15 us
  transfers between devices with their start and end apart: 3, of which 3 were waited for; matrix products, arithmetic and copies ran while one was open for 0% of the time, Pallas kernels for 9%

profile of v4, /device:TPU:0, one launch (start us, length us, event | category | flops | bytes accessed | tf_op | source)
XLA Modules:
  0.0 139.9 jit_solution(18334882001680033264)
XLA Ops:
  1.3 3.1 %project.1 = (bf16[32,2,64,128]{3,2,1,0:T(8,128)(2,1)S(1)}, bf16[128,2048]{1,0:T(8,128)(2,1)S(1)}) custom-call(s32[1]{0:T(128)S(6)} %copy.18.length, bf16[32,64,128]{2,1,0:T(8,128)(2,1)} %pair.1, f32[1,128]{1,0:T(1,128)} %bitcast.5, f32[1,128]{1,0:T(1,128)} %bitcast.9, bf16[128,256]{1,0:T(8,128)(2,1)} %lw.3, bf16[128,256]{1,0:T(8,128)(2,1)} %rw.3), custom_call_target="tpu_custom_call" | custom-call | flops 300000000 | bytes 3145728 | tf_op jit(solution)/shard_map/project/pallas_call | solution.py:42
  4.4 0.0 copy-start.4
  4.4 0.0 copy-start.5
  4.4 0.0 copy-start.6
  4.4 0.0 copy-start.7
  4.4 0.0 copy-start.8
  4.4 32.1 %all_to_all.30.recv = bf16[32,2,64,128]{3,2,1,0:T(8,128)(2,1)S(1)} all-to-all(bf16[32,2,64,128]{3,2,1,0:T(8,128)(2,1)S(1)} %get-tuple-element.35), channel_id=1, replica_groups=mesh['row'=8,'col'=4] {'row','col'}, dimensions={0} | all-to-all | bytes 2097152 | tf_op jit(solution)/shard_map/all_to_all | solution.py:68
  36.5 0.0 copy-start.9
  36.5 0.0 copy-start.11
  36.5 0.0 copy-start.12
  36.5 1.5 %multiply.1 = (bf16[32,64,128]{2,1,0:T(8,128)(2,1)}, bf16[4,256,256]{2,1,0:T(8,128)(2,1)S(1)}, bf16[4,256,256]{2,1,0:T(8,128)(2,1)S(1)}) custom-call(bf16[32,2,64,128]{3,2,1,0:T(8,128)(2,1)S(1)} %all_to_all.30.recv), custom_call_target="tpu_custom_call" | custom-call | flops 200000000 | bytes 3145728 | tf_op jit(solution)/shard_map/multiply/pallas_call | solution.py:42
  38.0 4.6 %all-to-all-start.1 = ((bf16[32,64,128]{2,1,0:T(8,128)(2,1)}), bf16[32,64,128]{2,1,0:T(8,128)(2,1)S(1)}, u32[]{:S(2)}, u32[]{:S(2)}) async-start(bf16[32,64,128]{2,1,0:T(8,128)(2,1)} %get-tuple-element.36), calls=%async_computation.1 | async-start | bytes 1048576 | tf_op jit(solution)/shard_map/all_to_all | solution.py:68
  42.5 0.0 copy-done.4
  42.5 0.0 copy-done.5
  42.5 0.0 copy-done.6
  42.6 0.0 copy-done.7
  42.6 0.0 copy-done.8
  42.6 2.6 %prepare.1 = (f32[128,2048]{1,0:T(8,128)S(1)}, bf16[128,2048]{1,0:T(8,128)(2,1)S(1)}, bf16[4,128,2048]{2,1,0:T(8,128)(2,1)S(1)}, f32[128,2048]{1,0:T(8,128)S(1)}, f32[8,2048]{1,0:T(8,128)S(1)}) custom-call(s32[1]{0:T(128)S(6)} %copy.18.length, bf16[32,64,128]{2,1,0:T(8,128)(2,1)S(1)} %copy-done.4, bf16[32,64,128]{2,1,0:T(8,128)(2,1)S(1)} %copy-done.5, ...), custom_call_target="tpu_custom_call" | custom-call | flops 400000000 | bytes 9437184 | tf_op jit(solution)/shard_map/prepare/pallas_call | solution.py:42
  45.2 0.0 copy-start
  45.2 1.0 copy-done
  46.1 0.0 copy-start.1
  46.2 1.3 copy-done.1
  47.5 0.0 copy-start.2
  47.5 0.8 copy-done.2
  48.3 0.0 copy-start.3
  48.3 1.0 copy-done.3
  49.3 7.5 %all-to-all-done.1.recv = bf16[32,64,128]{2,1,0:T(8,128)(2,1)S(1)} async-done(((bf16[32,64,128]{2,1,0:T(8,128)(2,1)}), bf16[32,64,128]{2,1,0:T(8,128)(2,1)S(1)}, u32[]{:S(2)}, u32[]{:S(2)}) %all-to-all-start.1) | async-done | bytes 524320 | tf_op jit(solution)/shard_map/all_to_all | solution.py:68
  56.8 0.0 copy-done.9
  56.8 0.0 copy-done.11
  56.8 0.0 copy-done.12
  56.8 3.3 %middle.1 = (bf16[32,64,128]{2,1,0:T(8,128)(2,1)S(1)}, f32[128,2048]{1,0:T(8,128)}, bf16[128,2048]{1,0:T(8,128)(2,1)}, bf16[128,2048]{1,0:T(8,128)(2,1)}, f32[2,128,128]{2,1,0:T(8,128)S(1)}) custom-call(bf16[32,64,128]{2,1,0:T(8,128)(2,1)S(1)} %all-to-all-done.1.recv, f32[128,2048]{1,0:T(8,128)} %copy-done, bf16[128,2048]{1,0:T(8,128)(2,1)} %copy-done.2, ...), custom_call_target="tpu_custom_call" | custom-call | flops 200000000 | bytes 6291456 | tf_op jit(solution)/shard_map/middle/pallas_call | solution.py:42
  60.1 18.2 %all_to_all.31.recv = bf16[32,64,128]{2,1,0:T(8,128)(2,1)S(1)} all-to-all(bf16[32,64,128]{2,1,0:T(8,128)(2,1)S(1)} %get-tuple-element.45), channel_id=1, replica_groups=mesh['row'=8,'col'=4] {'row','col'}, dimensions={0} | all-to-all | bytes 1048576 | tf_op jit(solution)/shard_map/all_to_all | solution.py:68
  78.3 1.9 %multiply_back.1 = bf16[32,2,64,128]{3,2,1,0:T(8,128)(2,1)} custom-call(bf16[32,64,128]{2,1,0:T(8,128)(2,1)S(1)} %all_to_all.31.recv, bf16[4,256,256]{2,1,0:T(8,128)(2,1)S(1)} %get-tuple-element.46.left, bf16[4,256,256]{2,1,0:T(8,128)(2,1)S(1)} %get-tuple-element.47.right), custom_call_target="tpu_custom_call" | custom-call | flops 300000000 | bytes 3145728 | tf_op jit(solution)/shard_map/multiply_back/pallas_call | solution.py:42
  80.2 4.2 %all-to-all-start.3 = ((bf16[32,2,64,128]{3,2,1,0:T(8,128)(2,1)}), bf16[32,2,64,128]{3,2,1,0:T(8,128)(2,1)S(1)}, u32[]{:S(2)}, u32[]{:S(2)}) async-start(bf16[32,2,64,128]{3,2,1,0:T(8,128)(2,1)} %multiply_back.1), calls=%async_computation.3 | async-start | bytes 2097152 | tf_op jit(solution)/shard_map/all_to_all | solution.py:68
  84.4 4.6 %settle.1 = (bf16[32,64,128]{2,1,0:T(8,128)(2,1)}, bf16[128,2048]{1,0:T(8,128)(2,1)}, f32[2,128,128]{2,1,0:T(8,128)S(1)}, f32[8,128]{1,0:T(8,128)S(1)}) custom-call(f32[128,2048]{1,0:T(8,128)} %get-tuple-element.40.outer_h, f32[128,2048]{1,0:T(8,128)} %copy-done, bf16[128,2048]{1,0:T(8,128)(2,1)} %copy-done.2, bf16[128,2048]{1,0:T(8,128)(2,1)} %get-tuple-element.41.og_h, ...), custom_call_target="tpu_custom_call" | custom-call | flops 200000000 | bytes 4194304 | tf_op jit(solution)/shard_map/settle/pallas_call | solution.py:42
  88.9 20.4 %all-to-all-done.3.recv = bf16[32,2,64,128]{3,2,1,0:T(8,128)(2,1)S(1)} async-done(((bf16[32,2,64,128]{3,2,1,0:T(8,128)(2,1)}), bf16[32,2,64,128]{3,2,1,0:T(8,128)(2,1)S(1)}, u32[]{:S(2)}, u32[]{:S(2)}) %all-to-all-start.3) | async-done | bytes 1048608 | tf_op jit(solution)/shard_map/all_to_all | solution.py:68
  109.3 0.0 copy-start.10
  109.3 3.7 %finish.1 = (bf16[768,128]{1,0:T(8,128)(2,1)}, bf16[2,256,2048]{2,1,0:T(8,128)(2,1)}) custom-call(bf16[32,2,64,128]{3,2,1,0:T(8,128)(2,1)S(1)} %all-to-all-done.3.recv, bf16[4,128,2048]{2,1,0:T(8,128)(2,1)} %copy-done.1, bf16[128,2048]{1,0:T(8,128)(2,1)S(1)} %get-tuple-element.37.nt_in.nt, f32[2,128,128]{2,1,0:T(8,128)S(1)} %get-tuple-element.49.early), custom_call_target="tpu_custom_call" | custom-call | flops 300000000 | bytes 8388608 | tf_op jit(solution)/shard_map/finish/pallas_call | solution.py:42
  113.0 4.6 %all-to-all-start.4 = ((bf16[32,24,128]{2,1,0:T(8,128)(2,1)}), bf16[32,24,128]{2,1,0:T(8,128)(2,1)S(1)}, u32[]{:S(2)}, u32[]{:S(2)}) async-start(bf16[32,24,128]{2,1,0:T(8,128)(2,1)} %bitcast.4), calls=%async_computation.4 | async-start | bytes 393216 | tf_op jit(solution)/shard_map/all_to_all | solution.py:68
  117.6 0.0 copy-done.10
  117.6 5.4 %close.1 = (bf16[32,64,128]{2,1,0:T(8,128)(2,1)}, bf16[8,128]{1,0:T(8,128)(2,1)S(1)}) custom-call(bf16[2,256,2048]{2,1,0:T(8,128)(2,1)} %get-tuple-element.50.comb_h, bf16[128,2048]{1,0:T(8,128)(2,1)} %get-tuple-element.51.gg_h, f32[128,2048]{1,0:T(8,128)} %copy-done.3, f32[8,2048]{1,0:T(8,128)S(1)} %get-tuple-element.53.scale, f32[1,128]{1,0:T(1,128)S(1)} %bitcast.6, ...), custom_call_target="tpu_custom_call" | custom-call | flops 300000000 | bytes 6291456 | tf_op jit(solution)/shard_map/close/pallas_call | solution.py:42
  123.0 3.9 %all-to-all-done.4.recv = bf16[32,24,128]{2,1,0:T(8,128)(2,1)S(1)} async-done(((bf16[32,24,128]{2,1,0:T(8,128)(2,1)}), bf16[32,24,128]{2,1,0:T(8,128)(2,1)S(1)}, u32[]{:S(2)}, u32[]{:S(2)}) %all-to-all-start.4) | async-done | bytes 196640 | tf_op jit(solution)/shard_map/all_to_all | solution.py:68
  126.9 0.1 add_up.1
  127.0 12.2 %all_to_all.32.recv = bf16[32,32,128]{2,1,0:T(8,128)(2,1)S(1)} all-to-all(bf16[32,32,128]{2,1,0:T(8,128)(2,1)S(1)} %add_up.1), channel_id=1, replica_groups=mesh['row'=8,'col'=4] {'row','col'}, dimensions={0} | all-to-all | bytes 524288 | tf_op jit(solution)/shard_map/all_to_all | solution.py:68
  139.2 0.8 deliver.1
Async XLA Ops:
  4.4 38.2 %copy-start.4 = (bf16[32,64,128]{2,1,0:T(8,128)(2,1)S(1)}, bf16[32,64,128]{2,1,0:T(8,128)(2,1)}, u32[]{:S(2)}) copy-start(bf16[32,64,128]{2,1,0:T(8,128)(2,1)} %pair.1) | copy-start | bytes 1572868
  4.4 38.2 %copy-start.5 = (bf16[32,64,128]{2,1,0:T(8,128)(2,1)S(1)}, bf16[32,64,128]{2,1,0:T(8,128)(2,1)}, u32[]{:S(2)}) copy-start(bf16[32,64,128]{2,1,0:T(8,128)(2,1)} %cot.1) | copy-start | bytes 1572868
  4.4 38.2 %copy-start.6 = (bf16[128,256]{1,0:T(8,128)(2,1)S(1)}, bf16[128,256]{1,0:T(8,128)(2,1)}, u32[]{:S(2)}) copy-start(bf16[128,256]{1,0:T(8,128)(2,1)} %lw.3) | copy-start | bytes 196612
  4.4 38.2 %copy-start.7 = (bf16[128,256]{1,0:T(8,128)(2,1)S(1)}, bf16[128,256]{1,0:T(8,128)(2,1)}, u32[]{:S(2)}) copy-start(bf16[128,256]{1,0:T(8,128)(2,1)} %rw.3) | copy-start | bytes 196612
  4.4 38.1 %copy-start.8 = (bf16[128,128]{1,0:T(8,128)(2,1)S(1)}, bf16[128,128]{1,0:T(8,128)(2,1)}, u32[]{:S(2)}) copy-start(bf16[128,128]{1,0:T(8,128)(2,1)} %gw.3) | copy-start | bytes 98308
  36.5 20.3 %copy-start.9 = (bf16[128,128]{1,0:T(8,128)(2,1)S(1)}, bf16[128,128]{1,0:T(8,128)(2,1)}, u32[]{:S(2)}) copy-start(bf16[128,128]{1,0:T(8,128)(2,1)} %ow.1) | copy-start | bytes 98308
  36.5 20.3 %copy-start.11 = (f32[128]{0:T(128)S(1)}, f32[128]{0:T(128)}, u32[]{:S(2)}) copy-start(f32[128]{0:T(128)} %param.19) | copy-start | bytes 1540
  36.5 20.3 %copy-start.12 = (f32[128]{0:T(128)S(1)}, f32[128]{0:T(128)}, u32[]{:S(2)}) copy-start(f32[128]{0:T(128)} %param.20) | copy-start | bytes 1540
  38.0 18.8 %all-to-all-start.1 = ((bf16[32,64,128]{2,1,0:T(8,128)(2,1)}), bf16[32,64,128]{2,1,0:T(8,128)(2,1)S(1)}, u32[]{:S(2)}, u32[]{:S(2)}) async-start(bf16[32,64,128]{2,1,0:T(8,128)(2,1)} %get-tuple-element.36), calls=%async_computation.1 | async-start | bytes 1048576 | tf_op jit(solution)/shard_map/all_to_all | solution.py:68
  45.2 1.0 copy-start
  46.1 1.3 copy-start.1
  47.5 0.8 copy-start.2
  48.3 1.0 copy-start.3
  80.2 29.1 %all-to-all-start.3 = ((bf16[32,2,64,128]{3,2,1,0:T(8,128)(2,1)}), bf16[32,2,64,128]{3,2,1,0:T(8,128)(2,1)S(1)}, u32[]{:S(2)}, u32[]{:S(2)}) async-start(bf16[32,2,64,128]{3,2,1,0:T(8,128)(2,1)} %multiply_back.1), calls=%async_computation.3 | async-start | bytes 2097152 | tf_op jit(solution)/shard_map/all_to_all | solution.py:68
  109.3 8.3 %copy-start.10 = (f32[128]{0:T(128)S(1)}, f32[128]{0:T(128)}, u32[]{:S(2)}) copy-start(f32[128]{0:T(128)} %param.14) | copy-start | bytes 1540
  113.0 13.9 %all-to-all-start.4 = ((bf16[32,24,128]{2,1,0:T(8,128)(2,1)}), bf16[32,24,128]{2,1,0:T(8,128)(2,1)S(1)}, u32[]{:S(2)}, u32[]{:S(2)}) async-start(bf16[32,24,128]{2,1,0:T(8,128)(2,1)} %bitcast.4), calls=%async_computation.4 | async-start | bytes 393216 | tf_op jit(solution)/shard_map/all_to_all | solution.py:68

commit v5 on v4

--- a/solution.py
+++ b/solution.py
@@ -17,7 +17,7 @@
 VMEM = pl.BlockSpec(memory_space=pltpu.VMEM)
 SMEM = pl.BlockSpec(memory_space=pltpu.SMEM)
 HBM = pl.BlockSpec(memory_space=pltpu.HBM)
-GROUPS = 4
+GROUPS = 2
 
 
 def dot(a, b, dims=NN):
@@ -136,7 +136,7 @@
 
     for g in range(GROUPS):
         finish_all(tiles[2 * g : 2 * g + 2])
-        lax.fori_loop(g * step_rows, (g + 1) * step_rows, step, 0, unroll=4)
+        lax.fori_loop(g * step_rows, (g + 1) * step_rows, step, 0, unroll=8)
 
     def pack(d, carry):
         for k in range(per // half):
@@ -259,7 +259,7 @@
     lax.fori_loop(0, n_dev, step, 0, unroll=4)
 
 
-def middle(half, hidden, recv, gate_h, cot_h, gain, bias, ow, send, outer_h, og_h, tn_h, sums, gate_in, cot_in, outer_out, og_out, tn_out, scr, owt, gb, sems, out_sems):
+def middle(half, hidden, recv, gate_h, cot_h, gain, bias, ow, send, tn_h, sums, gate_in, cot_in, tn_out, scr, gb, sems, out_sems):
     n_dev, per, _ = send.shape
     size = gate_in.shape[1] // GROUPS
     fetched = []
@@ -268,7 +268,6 @@
         fetched.append(begin(gate_h.at[:, at], gate_in.at[:, at], sems.at[2 * g]))
         fetched.append(begin(cot_h.at[:, at], cot_in.at[:, at], sems.at[2 * g + 1]))
     unpack(half, recv, scr)
-    owt[...] = flip(ow[...])
     gb[0] = column(gain[...])
     gb[1] = column(bias[...])
     sums[...] = jnp.zeros_like(sums)
@@ -279,12 +278,9 @@
         hat, scale = normal(scr[rows, :], 0)
         tn = (hat * gb[0] + gb[1]).astype(BF16)
         tn_out[:, at] = tn
-        outer = dot(owt[...], tn)
         gate = gate_in[:, at]
         up = cot_in[:, at].astype(F32)
-        outer_out[:, at] = outer
         og = (up * gate).astype(BF16)
-        og_out[:, at] = og
         tg = dot(ow[...], og)
         sums[0] += tg * hat
         sums[1] += tg
@@ -295,14 +291,12 @@
         return carry
 
     stored = []
-    saved = ((outer_out, outer_h), (og_out, og_h), (tn_out, tn_h))
     for g in range(GROUPS):
         finish_all(fetched[2 * g : 2 * g + 2])
         count = half // GROUPS
-        lax.fori_loop(g * count, (g + 1) * count, step, 0, unroll=4)
+        lax.fori_loop(g * count, (g + 1) * count, step, 0, unroll=8)
         at = span(g, size)
-        for k, (source, target) in enumerate(saved):
-            stored.append(begin(source.at[:, at], target.at[:, at], out_sems.at[3 * g + k]))
+        stored.append(begin(tn_out.at[:, at], tn_h.at[:, at], out_sems.at[g]))
 
     def pack(d, carry):
         for k in range(per // half):
@@ -318,18 +312,21 @@
     return jnp.sum(x.T, axis=0, keepdims=True)
 
 
-def settle(half, outer_h, gate_h, cot_h, og_h, tn_h, nt, sums, update, gg_h, early, norms, outer, gate, cot, og, tn, gg, sems):
-    pairs = ((outer_h, outer), (gate_h, gate), (cot_h, cot), (og_h, og), (tn_h, tn))
+def settle(half, gate_h, cot_h, tn_h, nt, sums, ow, update, gg_h, early, norms, gate, cot, og, tn, gg, owt, sems):
+    owt[...] = flip(ow[...])
+    pairs = ((gate_h, gate), (cot_h, cot), (tn_h, tn))
     finish_all([begin(a, b, sems.at[k]) for k, (a, b) in enumerate(pairs)])
 
     def step(p, carry):
         at = pl.ds(pl.multiple_of(p * LANES, LANES), LANES)
-        g, o = gate[:, at], outer[:, at]
+        g, up = gate[:, at], cot[:, at].astype(F32)
+        o = dot(owt[...], tn[:, at])
         tile = (g * o).T.astype(BF16)
         cols = update.shape[1]
         update[p] = tile[:cols]
         update[half + p] = tile[cols:]
-        gg[:, at] = (cot[:, at].astype(F32) * o * g * (1.0 - g)).astype(BF16)
+        og[:, at] = (up * g).astype(BF16)
+        gg[:, at] = (up * o * g * (1.0 - g)).astype(BF16)
         return carry
 
     lax.fori_loop(0, half, step, 0, unroll=2)
@@ -341,7 +338,15 @@
     stored.wait()
 
 
-def finish(half, hidden, recv, coef_h, nt, early, parts, comb_h, coef, comb, scr, total, sems, out_sems):
+def combine(half, hidden, scr, coef, side, p):
+    at = pl.ds(pl.multiple_of(p * LANES, LANES), LANES)
+    part = scr[side, pl.ds(p, hidden, stride=half + 1), :]
+    value = (part * coef[2 * side, :, at].astype(F32)).astype(BF16)
+    slope = (part * coef[2 * side + 1, :, at].astype(F32)).astype(BF16)
+    return jnp.concatenate([value, slope], axis=0)
+
+
+def finish(half, hidden, recv, coef_h, nt, early, parts, coef, comb, scr, total, sems):
     size = nt.shape[1] // GROUPS
     fetched = []
     for g in range(GROUPS):
@@ -352,20 +357,14 @@
 
     def step(p, carry):
         at = pl.ds(pl.multiple_of(p * LANES, LANES), LANES)
-        rows = pl.ds(p, hidden, stride=half + 1)
         for side in (0, 1):
-            part = scr[side, rows, :]
-            comb[side, :hidden, at] = (part * coef[2 * side, :, at].astype(F32)).astype(BF16)
-            comb[side, hidden:, at] = (part * coef[2 * side + 1, :, at].astype(F32)).astype(BF16)
-        return carry
-
-    stored = []
+            comb[side, :, at] = combine(half, hidden, scr, coef, side, p)
+        return carry
+
     for g in range(GROUPS):
         fetched[g].wait()
         count = half // GROUPS
-        lax.fori_loop(g * count, (g + 1) * count, step, 0, unroll=4)
-        at = span(g, size)
-        stored.append(begin(comb.at[:, :, at], comb_h.at[:, :, at], out_sems.at[g]))
+        lax.fori_loop(g * count, (g + 1) * count, step, 0, unroll=8)
         here = slice(g * size, (g + 1) * size)
         for side in (0, 1):
             part = dot(nt[:, here], comb[side, :, here], NT)
@@ -380,17 +379,18 @@
     parts[5 * c : base] = early[1].astype(BF16)
     if parts.shape[0] > base:
         parts[base:] = jnp.zeros((parts.shape[0] - base, LANES), BF16)
-    finish_all(stored)
-
-
-def close(half, comb_h, gg_h, hat_h, scale, gain, lw, rw, gw, early_norms, grad_pair, pairs, comb, gg, hat, sums, gb, sems):
+
+
+def close(half, hidden, recv, coef_h, gg_h, hat_h, scale, gain, lw, rw, gw, early_norms, grad_pair, pairs, coef, gg, hat, scr, sums, gb, sems):
     size = gg.shape[1] // GROUPS
     fetched = []
     for g in range(GROUPS):
         at = span(g, size)
-        fetched.append(begin(comb_h.at[:, :, at], comb.at[:, :, at], sems.at[3 * g]))
+        fetched.append(begin(coef_h.at[:, :, at], coef.at[:, :, at], sems.at[3 * g]))
         fetched.append(begin(gg_h.at[:, at], gg.at[:, at], sems.at[3 * g + 1]))
         fetched.append(begin(hat_h.at[:, at], hat.at[:, at], sems.at[3 * g + 2]))
+    for side in (0, 1):
+        unpack(half, recv, scr.at[side], side)
     gb[...] = column(gain[...])
     sums[...] = jnp.zeros_like(sums)
     cols = grad_pair.shape[1]
@@ -398,7 +398,9 @@
     def step(p, carry):
         at = pl.ds(pl.multiple_of(p * LANES, LANES), LANES)
         h = hat[:, at]
-        ng = dot(gw[...], gg[:, at]) + dot(lw[...], comb[0, :, at]) + dot(rw[...], comb[1, :, at])
+        ng = dot(gw[...], gg[:, at])
+        for side, w in ((0, lw), (1, rw)):
+            ng = ng + dot(w[...], combine(half, hidden, scr, coef, side, p))
         sums[0] += ng * h
         sums[1] += ng
         q = ng * gb[...]
@@ -470,7 +472,7 @@
     o_gain, o_bias = out_gain[None], out_bias[None]
     vm, dma = pltpu.VMEM, pltpu.SemaphoreType.DMA
     sq = (c, LANES)
-    rows = hidden * (half + 1)
+    rows = hidden * (half + 1) + 2 * half
 
     send, nt = call(
         functools.partial(project, half, hidden),
@@ -498,25 +500,23 @@
         "multiply", 200 * 10**6, 3 * 2**20,
     )(both)
     tri = exchange(send)
-    send, outer, og, tn, sums = call(
+    send, tn, sums = call(
         functools.partial(middle, half, hidden),
         (VMEM, HBM, HBM, VMEM, VMEM, VMEM),
-        [((n_dev, per, LANES), BF16, VMEM), ((c, wide), F32, HBM)]
-        + [((c, wide), BF16, HBM)] * 2 + [((2,) + sq, F32, VMEM)],
-        [vm((c, wide), F32), vm((c, wide), BF16), vm((c, wide), F32)]
-        + [vm((c, wide), BF16)] * 2 + [vm((rows, LANES), F32)]
-        + [vm((c, hidden), BF16), vm((2,) + sq, F32), dma((2 * GROUPS,)), dma((3 * GROUPS,))],
+        [((n_dev, per, LANES), BF16, VMEM), ((c, wide), BF16, HBM), ((2,) + sq, F32, VMEM)],
+        [vm((c, wide), F32)] + [vm((c, wide), BF16)] * 2 + [vm((rows, LANES), F32)]
+        + [vm((2,) + sq, F32), dma((2 * GROUPS,)), dma((GROUPS,))],
         "middle", 200 * 10**6, 6 * 2**20,
     )(tri, gate, cot, o_gain, o_bias, out_weight)
     grad = exchange(send)
     update, gg, early, early_norms = call(
         functools.partial(settle, half),
-        (HBM,) * 5 + (VMEM,) * 2,
+        (HBM,) * 3 + (VMEM,) * 3,
         [((rows_dev, cols_dev, c), BF16, VMEM), ((c, wide), BF16, HBM)]
         + [((2,) + sq, F32, VMEM), ((8, LANES), F32, VMEM)],
-        [vm((c, wide), F32)] * 2 + [vm((c, wide), BF16)] * 4 + [dma((6,))],
+        [vm((c, wide), F32)] + [vm((c, wide), BF16)] * 4 + [vm((c, hidden), BF16), dma((4,))],
         "settle", 200 * 10**6, 4 * 2**20,
-    )(outer, gate, cot, og, tn, nt, sums)
+    )(gate, cot, tn, nt, sums, out_weight)
     (send,) = call(
         functools.partial(multiply_back, n_row, n_col, half),
         (VMEM,) * 3,
@@ -527,23 +527,23 @@
     )(grad, left, right)
     back = exchange(send)
     share = -(-(5 * c + hidden) // (n_dev * 8)) * 8
-    parts, comb = call(
+    (parts,) = call(
         functools.partial(finish, half, hidden),
         (VMEM, HBM, VMEM, VMEM),
-        [((n_dev * share, LANES), BF16, VMEM), ((2, 2 * hidden, wide), BF16, HBM)],
+        [((n_dev * share, LANES), BF16, VMEM)],
         [vm((4, hidden, wide), BF16), vm((2, 2 * hidden, wide), BF16), vm((2, rows, LANES), F32)]
-        + [vm((2, c, 2 * hidden), F32), dma((GROUPS,)), dma((GROUPS,))],
+        + [vm((2, c, 2 * hidden), F32), dma((GROUPS,))],
         "finish", 300 * 10**6, 8 * 2**20,
     )(back, coef, nt, early)
     summed = exchange(parts.reshape(n_dev, share, LANES))
     grad_pair, pairs = call(
-        functools.partial(close, half),
-        (HBM,) * 3 + (VMEM,) * 6,
+        functools.partial(close, half, hidden),
+        (VMEM,) + (HBM,) * 3 + (VMEM,) * 6,
         [((rows_dev, cols_dev, c), BF16, VMEM), ((8, LANES), BF16, VMEM)],
-        [vm((2, 2 * hidden, wide), BF16), vm((c, wide), BF16), vm((c, wide), F32)]
-        + [vm((2,) + sq, F32), vm(sq, F32), dma((3 * GROUPS,))],
+        [vm((4, hidden, wide), BF16), vm((c, wide), BF16), vm((c, wide), F32)]
+        + [vm((2, rows, LANES), F32), vm((2,) + sq, F32), vm(sq, F32), dma((3 * GROUPS,))],
         "close", 300 * 10**6, 6 * 2**20,
-    )(comb, gg, hat, scale, gain, left_weight, right_weight, gate_weight, early_norms)
+    )(back, coef, gg, hat, scale, gain, left_weight, right_weight, gate_weight, early_norms)
     (send,) = call(
         functools.partial(add_up, 1.0 / tokens),
         (VMEM, VMEM),

time: 140 us -> 139 us (level)
  transfers between devices with their start and end apart: 3 -> 3, of which waited for: 3 -> 3; matrix products, arithmetic and copies ran while one was open for 0% -> 0% of each run, Pallas kernels for 9% -> 10%
where the time goes in v5:
time: 139 us; the launch traced here: 138 us
  blocking collectives  62.6 us (45%)
  waiting for transfers between devices  30.9 us (22%)
  Pallas kernels  25.9 us (19%)
  starting transfers between devices  13.3 us (10%)
  local copies, waits for them, and re-layouts  4.12 us (3%)
  between operations  1.48 us (1%)
    all_to_all x3, blocking collectives, exchange(): return lax.all_to_all(blocks, BOTH, split_axis=0, concat_axis=0, tiled=True)  62.6 us
    all_to_all x3, waiting for transfers between devices, exchange(): return lax.all_to_all(blocks, BOTH, split_axis=0, concat_axis=0, tiled=True)  30.9 us
    pallas_call x10, Pallas kernels, placed(): run(*[pltpu.with_memory_space_constraint(x, pltpu.HBM) if spec is HBM els...  25.9 us
    all_to_all x3, starting transfers between devices, exchange(): return lax.all_to_all(blocks, BOTH, split_axis=0, concat_axis=0, tiled=True)  13.3 us
    unnamed x26, local copies, waits for them, and re-layouts  4.12 us
  transfers between devices with their start and end apart: 3, of which 3 were waited for; matrix products, arithmetic and copies ran while one was open for 0% of the time, Pallas kernels for 10%

profile of v5, /device:TPU:0, one launch (start us, length us, event | category | flops | bytes accessed | tf_op | source)
XLA Modules:
  0.0 138.3 jit_solution(10151102036718897043)
XLA Ops:
  1.3 2.5 %project.1 = (bf16[32,2,64,128]{3,2,1,0:T(8,128)(2,1)S(1)}, bf16[128,2048]{1,0:T(8,128)(2,1)S(1)}) custom-call(s32[1]{0:T(128)S(6)} %copy.18.length, bf16[32,64,128]{2,1,0:T(8,128)(2,1)} %pair.1, f32[1,128]{1,0:T(1,128)} %bitcast.5, f32[1,128]{1,0:T(1,128)} %bitcast.9, bf16[128,256]{1,0:T(8,128)(2,1)} %lw.3, bf16[128,256]{1,0:T(8,128)(2,1)} %rw.3), custom_call_target="tpu_custom_call" | custom-call | flops 300000000 | bytes 3145728 | tf_op jit(solution)/shard_map/project/pallas_call | solution.py:42
  3.8 0.0 copy-start.4
  3.8 0.0 copy-start.5
  3.8 0.0 copy-start.6
  3.8 0.0 copy-start.7
  3.8 0.0 copy-start.9
  3.9 32.1 %all_to_all.30.recv = bf16[32,2,64,128]{3,2,1,0:T(8,128)(2,1)S(1)} all-to-all(bf16[32,2,64,128]{3,2,1,0:T(8,128)(2,1)S(1)} %get-tuple-element.34), channel_id=1, replica_groups=mesh['row'=8,'col'=4] {'row','col'}, dimensions={0} | all-to-all | bytes 2097152 | tf_op jit(solution)/shard_map/all_to_all | solution.py:68
  35.9 0.0 copy-start.8
  35.9 0.0 copy-start.11
  35.9 0.0 copy-start.12
  35.9 1.5 %multiply.1 = (bf16[32,64,128]{2,1,0:T(8,128)(2,1)}, bf16[4,256,256]{2,1,0:T(8,128)(2,1)S(1)}, bf16[4,256,256]{2,1,0:T(8,128)(2,1)S(1)}) custom-call(bf16[32,2,64,128]{3,2,1,0:T(8,128)(2,1)S(1)} %all_to_all.30.recv), custom_call_target="tpu_custom_call" | custom-call | flops 200000000 | bytes 3145728 | tf_op jit(solution)/shard_map/multiply/pallas_call | solution.py:42
  37.4 4.6 %all-to-all-start.1 = ((bf16[32,64,128]{2,1,0:T(8,128)(2,1)}), bf16[32,64,128]{2,1,0:T(8,128)(2,1)S(1)}, u32[]{:S(2)}, u32[]{:S(2)}) async-start(bf16[32,64,128]{2,1,0:T(8,128)(2,1)} %get-tuple-element.35), calls=%async_computation.1 | async-start | bytes 1048576 | tf_op jit(solution)/shard_map/all_to_all | solution.py:68
  42.0 0.0 copy-done.4
  42.0 0.0 copy-done.5
  42.0 0.0 copy-done.6
  42.0 0.0 copy-done.7
  42.0 0.0 copy-done.9
  42.0 2.6 %prepare.1 = (f32[128,2048]{1,0:T(8,128)S(1)}, bf16[128,2048]{1,0:T(8,128)(2,1)S(1)}, bf16[4,128,2048]{2,1,0:T(8,128)(2,1)S(1)}, f32[128,2048]{1,0:T(8,128)S(1)}, f32[8,2048]{1,0:T(8,128)S(1)}) custom-call(s32[1]{0:T(128)S(6)} %copy.18.length, bf16[32,64,128]{2,1,0:T(8,128)(2,1)S(1)} %copy-done.4, bf16[32,64,128]{2,1,0:T(8,128)(2,1)S(1)} %copy-done.5, ...), custom_call_target="tpu_custom_call" | custom-call | flops 400000000 | bytes 9437184 | tf_op jit(solution)/shard_map/prepare/pallas_call | solution.py:42
  44.6 0.0 copy-start
  44.6 1.3 copy-done
  45.9 0.0 copy-start.1
  45.9 1.0 copy-done.1
  46.9 0.0 copy-start.2
  46.9 0.8 copy-done.2
  47.7 0.0 copy-start.3
  47.7 1.0 copy-done.3
  48.7 7.5 %all-to-all-done.1.recv = bf16[32,64,128]{2,1,0:T(8,128)(2,1)S(1)} async-done(((bf16[32,64,128]{2,1,0:T(8,128)(2,1)}), bf16[32,64,128]{2,1,0:T(8,128)(2,1)S(1)}, u32[]{:S(2)}, u32[]{:S(2)}) %all-to-all-start.1) | async-done | bytes 524320 | tf_op jit(solution)/shard_map/all_to_all | solution.py:68
  56.2 0.0 copy-done.8
  56.2 0.0 copy-done.11
  56.2 0.0 copy-done.12
  56.2 2.9 %middle.1 = (bf16[32,64,128]{2,1,0:T(8,128)(2,1)S(1)}, bf16[128,2048]{1,0:T(8,128)(2,1)}, f32[2,128,128]{2,1,0:T(8,128)S(1)}) custom-call(bf16[32,64,128]{2,1,0:T(8,128)(2,1)S(1)} %all-to-all-done.1.recv, f32[128,2048]{1,0:T(8,128)} %copy-done.1, bf16[128,2048]{1,0:T(8,128)(2,1)} %copy-done.2, f32[1,128]{1,0:T(1,128)S(1)} %bitcast.7, f32[1,128]{1,0:T(1,128)S(1)} %bitcast.8, ...), custom_call_target="tpu_custom_call" | custom-call | flops 200000000 | bytes 6291456 | tf_op jit(solution)/shard_map/middle/pallas_call | solution.py:42
  59.1 18.2 %all_to_all.31.recv = bf16[32,64,128]{2,1,0:T(8,128)(2,1)S(1)} all-to-all(bf16[32,64,128]{2,1,0:T(8,128)(2,1)S(1)} %get-tuple-element.39), channel_id=1, replica_groups=mesh['row'=8,'col'=4] {'row','col'}, dimensions={0} | all-to-all | bytes 1048576 | tf_op jit(solution)/shard_map/all_to_all | solution.py:68
  77.3 1.9 %multiply_back.1 = bf16[32,2,64,128]{3,2,1,0:T(8,128)(2,1)} custom-call(bf16[32,64,128]{2,1,0:T(8,128)(2,1)S(1)} %all_to_all.31.recv, bf16[4,256,256]{2,1,0:T(8,128)(2,1)S(1)} %get-tuple-element.40.left, bf16[4,256,256]{2,1,0:T(8,128)(2,1)S(1)} %get-tuple-element.41.right), custom_call_target="tpu_custom_call" | custom-call | flops 300000000 | bytes 3145728 | tf_op jit(solution)/shard_map/multiply_back/pallas_call | solution.py:42
  79.2 4.2 %all-to-all-start.3 = ((bf16[32,2,64,128]{3,2,1,0:T(8,128)(2,1)}), bf16[32,2,64,128]{3,2,1,0:T(8,128)(2,1)S(1)}, u32[]{:S(2)}, u32[]{:S(2)}) async-start(bf16[32,2,64,128]{3,2,1,0:T(8,128)(2,1)} %multiply_back.1), calls=%async_computation.3 | async-start | bytes 2097152 | tf_op jit(solution)/shard_map/all_to_all | solution.py:68
  83.4 5.1 %settle.1 = (bf16[32,64,128]{2,1,0:T(8,128)(2,1)}, bf16[128,2048]{1,0:T(8,128)(2,1)}, f32[2,128,128]{2,1,0:T(8,128)S(1)}, f32[8,128]{1,0:T(8,128)S(1)}) custom-call(f32[128,2048]{1,0:T(8,128)} %copy-done.1, bf16[128,2048]{1,0:T(8,128)(2,1)} %copy-done.2, bf16[128,2048]{1,0:T(8,128)(2,1)} %get-tuple-element.36.tn_h, ...), custom_call_target="tpu_custom_call" | custom-call | flops 200000000 | bytes 4194304 | tf_op jit(solution)/shard_map/settle/pallas_call | solution.py:42
  88.5 19.8 %all-to-all-done.3.recv = bf16[32,2,64,128]{3,2,1,0:T(8,128)(2,1)S(1)} async-done(((bf16[32,2,64,128]{3,2,1,0:T(8,128)(2,1)}), bf16[32,2,64,128]{3,2,1,0:T(8,128)(2,1)S(1)}, u32[]{:S(2)}, u32[]{:S(2)}) %all-to-all-start.3) | async-done | bytes 1048608 | tf_op jit(solution)/shard_map/all_to_all | solution.py:68
  108.3 0.0 copy-start.10
  108.3 3.0 %finish.1 = bf16[768,128]{1,0:T(8,128)(2,1)} custom-call(bf16[32,2,64,128]{3,2,1,0:T(8,128)(2,1)S(1)} %all-to-all-done.3.recv, bf16[4,128,2048]{2,1,0:T(8,128)(2,1)} %copy-done, bf16[128,2048]{1,0:T(8,128)(2,1)S(1)} %get-tuple-element.31.nt_in.nt, f32[2,128,128]{2,1,0:T(8,128)S(1)} %get-tuple-element.48.early), custom_call_target="tpu_custom_call" | custom-call | flops 300000000 | bytes 8388608 | tf_op jit(solution)/shard_map/finish/pallas_call | solution.py:42
  111.3 4.6 %all-to-all-start.4 = ((bf16[32,24,128]{2,1,0:T(8,128)(2,1)}), bf16[32,24,128]{2,1,0:T(8,128)(2,1)S(1)}, u32[]{:S(2)}, u32[]{:S(2)}) async-start(bf16[32,24,128]{2,1,0:T(8,128)(2,1)} %bitcast.4), calls=%async_computation.4 | async-start | bytes 393216 | tf_op jit(solution)/shard_map/all_to_all | solution.py:68
  115.9 0.0 copy-done.10
  115.9 5.7 %close.1 = (bf16[32,64,128]{2,1,0:T(8,128)(2,1)}, bf16[8,128]{1,0:T(8,128)(2,1)S(1)}) custom-call(bf16[32,2,64,128]{3,2,1,0:T(8,128)(2,1)S(1)} %all-to-all-done.3.recv, bf16[4,128,2048]{2,1,0:T(8,128)(2,1)} %copy-done, bf16[128,2048]{1,0:T(8,128)(2,1)} %get-tuple-element.43.gg_h, f32[128,2048]{1,0:T(8,128)} %copy-done.3, ...), custom_call_target="tpu_custom_call" | custom-call | flops 300000000 | bytes 6291456 | tf_op jit(solution)/shard_map/close/pallas_call | solution.py:42
  121.6 3.6 %all-to-all-done.4.recv = bf16[32,24,128]{2,1,0:T(8,128)(2,1)S(1)} async-done(((bf16[32,24,128]{2,1,0:T(8,128)(2,1)}), bf16[32,24,128]{2,1,0:T(8,128)(2,1)S(1)}, u32[]{:S(2)}, u32[]{:S(2)}) %all-to-all-start.4) | async-done | bytes 196640 | tf_op jit(solution)/shard_map/all_to_all | solution.py:68
  125.2 0.1 add_up.1
  125.3 12.3 %all_to_all.32.recv = bf16[32,32,128]{2,1,0:T(8,128)(2,1)S(1)} all-to-all(bf16[32,32,128]{2,1,0:T(8,128)(2,1)S(1)} %add_up.1), channel_id=1, replica_groups=mesh['row'=8,'col'=4] {'row','col'}, dimensions={0} | all-to-all | bytes 524288 | tf_op jit(solution)/shard_map/all_to_all | solution.py:68
  137.6 0.8 deliver.1
Async XLA Ops:
  3.8 38.2 %copy-start.4 = (bf16[32,64,128]{2,1,0:T(8,128)(2,1)S(1)}, bf16[32,64,128]{2,1,0:T(8,128)(2,1)}, u32[]{:S(2)}) copy-start(bf16[32,64,128]{2,1,0:T(8,128)(2,1)} %pair.1) | copy-start | bytes 1572868
  3.8 38.2 %copy-start.5 = (bf16[32,64,128]{2,1,0:T(8,128)(2,1)S(1)}, bf16[32,64,128]{2,1,0:T(8,128)(2,1)}, u32[]{:S(2)}) copy-start(bf16[32,64,128]{2,1,0:T(8,128)(2,1)} %cot.1) | copy-start | bytes 1572868
  3.8 38.1 %copy-start.6 = (bf16[128,256]{1,0:T(8,128)(2,1)S(1)}, bf16[128,256]{1,0:T(8,128)(2,1)}, u32[]{:S(2)}) copy-start(bf16[128,256]{1,0:T(8,128)(2,1)} %lw.3) | copy-start | bytes 196612
  3.8 38.1 %copy-start.7 = (bf16[128,256]{1,0:T(8,128)(2,1)S(1)}, bf16[128,256]{1,0:T(8,128)(2,1)}, u32[]{:S(2)}) copy-start(bf16[128,256]{1,0:T(8,128)(2,1)} %rw.3) | copy-start | bytes 196612
  3.8 38.1 %copy-start.9 = (bf16[128,128]{1,0:T(8,128)(2,1)S(1)}, bf16[128,128]{1,0:T(8,128)(2,1)}, u32[]{:S(2)}) copy-start(bf16[128,128]{1,0:T(8,128)(2,1)} %gw.3) | copy-start | bytes 98308
  35.9 20.3 %copy-start.8 = (bf16[128,128]{1,0:T(8,128)(2,1)S(1)}, bf16[128,128]{1,0:T(8,128)(2,1)}, u32[]{:S(2)}) copy-start(bf16[128,128]{1,0:T(8,128)(2,1)} %ow.3) | copy-start | bytes 98308
  35.9 20.3 %copy-start.11 = (f32[128]{0:T(128)S(1)}, f32[128]{0:T(128)}, u32[]{:S(2)}) copy-start(f32[128]{0:T(128)} %param.19) | copy-start | bytes 1540
  35.9 20.3 %copy-start.12 = (f32[128]{0:T(128)S(1)}, f32[128]{0:T(128)}, u32[]{:S(2)}) copy-start(f32[128]{0:T(128)} %param.20) | copy-start | bytes 1540
  37.4 18.8 %all-to-all-start.1 = ((bf16[32,64,128]{2,1,0:T(8,128)(2,1)}), bf16[32,64,128]{2,1,0:T(8,128)(2,1)S(1)}, u32[]{:S(2)}, u32[]{:S(2)}) async-start(bf16[32,64,128]{2,1,0:T(8,128)(2,1)} %get-tuple-element.35), calls=%async_computation.1 | async-start | bytes 1048576 | tf_op jit(solution)/shard_map/all_to_all | solution.py:68
  44.6 1.3 copy-start
  45.9 1.0 copy-start.1
  46.9 0.8 copy-start.2
  47.7 1.0 copy-start.3
  79.2 29.1 %all-to-all-start.3 = ((bf16[32,2,64,128]{3,2,1,0:T(8,128)(2,1)}), bf16[32,2,64,128]{3,2,1,0:T(8,128)(2,1)S(1)}, u32[]{:S(2)}, u32[]{:S(2)}) async-start(bf16[32,2,64,128]{3,2,1,0:T(8,128)(2,1)} %multiply_back.1), calls=%async_computation.3 | async-start | bytes 2097152 | tf_op jit(solution)/shard_map/all_to_all | solution.py:68
  108.3 7.6 %copy-start.10 = (f32[128]{0:T(128)S(1)}, f32[128]{0:T(128)}, u32[]{:S(2)}) copy-start(f32[128]{0:T(128)} %param.14) | copy-start | bytes 1540
  111.3 13.9 %all-to-all-start.4 = ((bf16[32,24,128]{2,1,0:T(8,128)(2,1)}), bf16[32,24,128]{2,1,0:T(8,128)(2,1)S(1)}, u32[]{:S(2)}, u32[]{:S(2)}) async-start(bf16[32,24,128]{2,1,0:T(8,128)(2,1)} %bitcast.4), calls=%async_computation.4 | async-start | bytes 393216 | tf_op jit(solution)/shard_map/all_to_all | solution.py:68
